TPU v7x, 128 devices: a whole 4x4x4 slice. The times are simulated.
128 devices in a mesh: rows: 16 (over y, z), seq: 8 (over x, core).
Axes of the slice: x: 4, y: 4, z: 4, core: 2. Of those that a mesh axis runs over, the one named last changes fastest.
Arguments:
- residual_in: bfloat16 [16, 2048, 3200], P('rows', 'seq'), may hold values from -6 to 6
- norm_gain: float32 [3200], replicated, may hold values from 0.1 to 1.9
- qkv_weight: bfloat16 [3200, 6144], P(None, 'seq')
- qk_gain: float32 [2, 2048], P(None, 'seq')
- out_weight: bfloat16 [2048, 3200], P('seq'), may hold values from -0.125 to 0.125
- layer_scale: float32 [3200], replicated, may hold values from 1 to 6
- segment_ids: int32 [16, 2048], P('rows', 'seq'), may hold values from 0 to 2, as said below
- pad_mask: int32 [16, 2048], P('rows', 'seq'), may hold values from 0 to 1, as said below
- ln_weight: float32 [12800], replicated, may hold values from 0.1 to 1.9
- ln_bias: float32 [12800], replicated, may hold values from -3 to 3
- fc_weight: bfloat16 [12800, 6144], P('rows'), may hold values from -0.0546875 to 0.0546875
- fc_bias: float32 [6144], replicated, may hold values from -3 to 3
- owner: int32 [16], replicated, may hold values from 0 to 15, each once
Outputs:
- features: bfloat16 [16, 512, 6144], P('rows', 'seq')
Inputs may be any that keep to these rules, and one draw needn't show every extreme that they name: `segment_ids`: within a row, segment ids never fall and change only at multiples of 1024 tokens; picture tokens carry ids below 2, padding tokens carry 2 and stand at the end of the row; the first tile is never padding. pad_mask is 0 exactly where segment_ids equals 2. `owner`: each index of rows owns exactly one row.
All inputs are finite; a program needn't handle non-finite values.
Results may differ from a plain program's by a relative error of at most 0.025.
Values may be sent and summed in bfloat16 or wider, within the bound.
A program may use at most 128 MiB of HBM per device.

v0:
```python
import jax
import jax.numpy as jnp
from jax import lax
from jax.sharding import PartitionSpec as P

D = 3200
HEAD_DIM = 128
HEADS = 16
GRID = 32


def attend_dense(query_norm, key_norm, value_half, row_segments, block_len, scale):
    length, heads_here = (query_norm.shape[0], query_norm.shape[1])
    block_count = length // block_len

    def one_block(packed):
        query_block, query_seg = packed
        scores = (
            jnp.einsum("qhd,khd->hqk", query_block, key_norm, preferred_element_type=jnp.float32)
            * scale
        )
        same_seg = (query_seg[:, None] == row_segments[None, :])[None]
        scores = jnp.where(same_seg, scores, -1e30)
        peak_val = jnp.max(scores, axis=-1, keepdims=True)
        exp_terms = jnp.exp(scores - peak_val)
        probs = (exp_terms / jnp.sum(exp_terms, axis=-1, keepdims=True)).astype(jnp.bfloat16)
        return jnp.einsum(
            "hqk,khd->qhd", probs, value_half, preferred_element_type=jnp.float32
        ).astype(jnp.bfloat16)

    blocks_out = lax.map(
        one_block,
        (
            query_norm.reshape(block_count, block_len, heads_here, HEAD_DIM),
            row_segments.reshape(block_count, block_len),
        ),
    )
    return blocks_out.reshape(length, heads_here * HEAD_DIM)


def per_device(
    residual_in,
    norm_gain,
    qkv_weight,
    qk_gain,
    out_weight,
    layer_scale,
    segment_ids,
    pad_mask,
    ln_weight,
    ln_bias,
    fc_weight,
    fc_bias,
    owner,
):
    tokens = residual_in[0].astype(jnp.float32)
    shard_rows = tokens.shape[0]
    normed = (
        tokens * lax.rsqrt(jnp.mean(tokens * tokens, axis=-1, keepdims=True) + 1e-06) * norm_gain
    ).astype(jnp.bfloat16)
    row_tokens, row_segments = (
        lax.all_gather(normed, "seq", axis=0, tiled=True),
        lax.all_gather(segment_ids[0].astype(jnp.bfloat16), "seq", axis=0, tiled=True),
    )
    length = row_tokens.shape[0]
    heads_here = qkv_weight.shape[1] // (3 * HEAD_DIM)
    projected = jnp.dot(row_tokens, qkv_weight, preferred_element_type=jnp.float32).reshape(
        length, heads_here, 3, HEAD_DIM
    )
    query_raw = projected[:, :, 0]
    key_raw = projected[:, :, 1]
    value_half = projected[:, :, 2].astype(jnp.bfloat16)
    query_sq, key_sq = lax.psum(
        (jnp.sum(query_raw * query_raw, axis=(1, 2)), jnp.sum(key_raw * key_raw, axis=(1, 2))),
        "seq",
    )
    norm_width = HEADS * HEAD_DIM
    gain_pair = qk_gain.reshape(2, heads_here, HEAD_DIM)
    query_norm = (
        query_raw * lax.rsqrt(query_sq / norm_width + 1e-06)[:, None, None] * gain_pair[0]
    ).astype(jnp.bfloat16)
    key_norm = (
        key_raw * lax.rsqrt(key_sq / norm_width + 1e-06)[:, None, None] * gain_pair[1]
    ).astype(jnp.bfloat16)
    block_len = min(512, length)
    scale = HEAD_DIM ** (-0.5)
    attended = attend_dense(query_norm, key_norm, value_half, row_segments, block_len, scale)
    piece = attended
    attn = lax.psum_scatter(
        jnp.dot(piece, out_weight, preferred_element_type=jnp.float32).astype(jnp.bfloat16),
        "seq",
        scatter_dimension=0,
        tiled=True,
    ).astype(jnp.float32)
    hidden = tokens + layer_scale * attn
    half_grid = GRID // 2
    lines = shard_rows // (2 * GRID)
    merged_count = shard_rows // 4
    merged = jnp.transpose(hidden.reshape(lines, 2, half_grid, 2, D), (0, 2, 1, 3, 4)).reshape(
        merged_count, 4 * D
    )
    centre = merged - jnp.mean(merged, axis=-1, keepdims=True)
    spread = jnp.mean(centre * centre, axis=-1, keepdims=True)
    merged_norm = (centre * lax.rsqrt(spread + 1e-05) * ln_weight + ln_bias).astype(jnp.bfloat16)
    merged_mask = (
        pad_mask[0]
        .reshape(lines, 2, half_grid, 2)[:, 0, :, 0]
        .reshape(merged_count)
        .astype(jnp.bfloat16)
    )
    row_count = lax.axis_size("rows")
    mask_spread = jnp.broadcast_to(merged_mask[:, None], (merged_count, row_count))
    slabs, slab_mask = (
        lax.all_to_all(merged_norm, "rows", split_axis=1, concat_axis=0, tiled=True),
        lax.all_to_all(mask_spread, "rows", split_axis=1, concat_axis=0, tiled=True),
    )
    owner_hot = (owner[None, :] == jnp.arange(row_count, dtype=jnp.int32)[:, None]).astype(
        jnp.bfloat16
    )
    ordered = jnp.einsum(
        "jp,pms->jms",
        owner_hot,
        slabs.reshape(row_count, merged_count, -1),
        preferred_element_type=jnp.float32,
    ).astype(jnp.bfloat16)
    ordered = ordered.reshape(row_count * merged_count, -1)
    ordered_mask = jnp.einsum(
        "jp,pms->jms",
        owner_hot,
        slab_mask.reshape(row_count, merged_count, 1),
        preferred_element_type=jnp.float32,
    )
    ordered_mask = ordered_mask.reshape(row_count * merged_count)
    piece = ordered
    summed = lax.psum_scatter(
        jnp.dot(piece, fc_weight, preferred_element_type=jnp.float32).astype(jnp.bfloat16),
        "rows",
        scatter_dimension=0,
        tiled=True,
    ).astype(jnp.float32)
    own_mask = lax.dynamic_slice_in_dim(
        ordered_mask, lax.axis_index("rows") * merged_count, merged_count, 0
    )
    result = jax.nn.gelu(summed + fc_bias, approximate=False) * own_mask[:, None]
    return result.astype(jnp.bfloat16)[None]


def solution(mesh):
    return jax.shard_map(
        per_device,
        mesh=mesh,
        in_specs=(
            P("rows", "seq", None),
            P(),
            P(None, "seq"),
            P(None, "seq"),
            P("seq", None),
            P(),
            P("rows", "seq"),
            P("rows", "seq"),
            P(),
            P(),
            P("rows", None),
            P(),
            P(),
        ),
        out_specs=P("rows", "seq", None),
        check_vma=False,
    )
```

profile of v0, /device:TPU:1, one launch (start us, length us, event | category | flops | bytes accessed | tf_op | source)
XLA Modules:
  0.0 465.9 jit_solution(8519050404227849196)
XLA Ops:
  6.5 2.0 fusion.27
  8.6 2.3 fusion.29
  11.0 0.6 copy-done.11
  11.6 11.9 %all-gather = bf16[1,2048]{1,0:T(2,128)(2,1)S(1)} all-gather(bf16[1,256]{1,0:T(2,128)(2,1)S(1)} %convert_element_type.68), channel_id=2, replica_groups=mesh['rows'=16,'seq'=8] {'seq'}, dimensions={1}, use_global_device_ids=true | all-gather | bytes 4608 | tf_op jit(solution)/shard_map/all_gather | solution.py:63
  23.5 60.7 %all-gather.3.cloned.1.call-done = bf16[2048,3200]{1,0:T(8,128)(2,1)} async-done(((bf16[256,3200]{1,0:T(8,128)(2,1)}), bf16[2048,3200]{1,0:T(8,128)(2,1)}) %all-gather.3.cloned.1.call-update) | async-done | bytes 13107216 | tf_op jit(solution)/shard_map/all_gather | solution.py:62
  84.3 15.7 %fusion.71 = f32[2048,768]{0,1:T(8,128)S(1)} fusion(bf16[2048,3200]{1,0:T(8,128)(2,1)} %all-gather.3.cloned.1.call-done, bf16[3200,768]{1,0:T(8,128)(2,1)} %param.17), kind=kOutput, calls=%fused_computation.91 | convolution fusion | flops 10066329600 | bytes 24313856 | tf_op jit(solution)/shard_map/dot_general | solution.py:67
  100.0 2.5 fusion.69
  102.5 0.1 slice.30
  102.6 2.9 copy.54
  105.6 1.9 fusion.30
  107.5 2.9 copy.53
  110.4 1.9 multiply_reduce_fusion.1
  112.3 21.0 %all-reduce = (f32[2048]{0:T(1024)S(1)}, f32[2048]{0:T(1024)S(1)}) all-reduce(f32[2048]{0:T(1024)S(1)} %multiply_reduce_fusion.1, f32[2048]{0:T(1024)S(1)} %fusion.30), channel_id=1, replica_groups=mesh['rows'=16,'seq'=8] {'seq'}, use_global_device_ids=true, to_apply=%region_2.0 | all-reduce | flops 4096 | bytes 32768 | tf_op jit(solution)/shard_map/psum | solution.py:73
  133.3 1.3 copy.55
  134.7 3.1 fusion.32
  137.8 1.3 multiply_convert_fusion
  139.1 56.9 %while.10 = (s32[]{:T(128)}, bf16[4,512,2,128]{3,2,1,0:T(2,128)(2,1)}, bf16[4,512]{1,0:T(4,128)(2,1)S(1)}, bf16[2048]{0:T(1024)(128)(2,1)S(1)}, bf16[4,512,2,128...) while((s32[]{:T(128)}, ...), condition=%wide.region_8.9_spmd, body=%wide.region_5.8_spmd.sunk | while | flops 1087506432 | bytes 22036568 | solution.py:31
  139.2 0.6 broadcast_compare_fusion.2
  139.8 7.7 %fusion.88 = (f32[2,512]{1,0:T(2,128)S(1)}, f32[2,512,2048]{2,1,0:T(8,128)}) fusion(pred[512,2048]{1,0:T(8,128)(4,1)S(1)} %broadcast_compare_fusion.2, bf16[2048,2,128]{2,0,1:T(8,128)(2,1)} %get-tuple-element.161, bf16[4,512,2,128]{3,1,0,2:T(8,128)(2,1)} %get-tuple-element.160, s32[]{:T(128)} %get-tuple-element.148), kind=kOutput, calls=%fused_computation.88.clone.1 | convolution fusion | flops 545261568 | bytes 10752512 | tf_op jit(solution)/shard_map/while/body/eval_jaxpr/sub | solution.py:25
  147.5 4.9 %fusion.89 = bf16[1,512,2,128]{3,1,2,0:T(8,128)(2,1)S(1)} fusion(bf16[2048,2,128]{2,0,1:T(8,128)(2,1)} %get-tuple-element.162, f32[2,512,2048]{2,1,0:T(8,128)} %get-tuple-element.138, f32[2,512]{1,0:T(2,128)S(1)} %get-tuple-element.139), kind=kOutput, calls=%fused_computation.10.clone.1 | convolution fusion | flops 541196288 | bytes 9703424 | tf_op jit(solution)/shard_map/while/body/eval_jaxpr/hqk,khd->qhd/dot_general | solution.py:27
  152.4 1.0 copy_dynamic-update-slice_fusion.2
  153.4 0.6 broadcast_compare_fusion.2
  154.0 7.7 %fusion.88 = (f32[2,512]{1,0:T(2,128)S(1)}, f32[2,512,2048]{2,1,0:T(8,128)}) fusion(pred[512,2048]{1,0:T(8,128)(4,1)S(1)} %broadcast_compare_fusion.2, bf16[2048,2,128]{2,0,1:T(8,128)(2,1)} %get-tuple-element.161, bf16[4,512,2,128]{3,1,0,2:T(8,128)(2,1)} %get-tuple-element.160, s32[]{:T(128)} %get-tuple-element.148), kind=kOutput, calls=%fused_computation.88.clone.1 | convolution fusion | flops 545261568 | bytes 10752512 | tf_op jit(solution)/shard_map/while/body/eval_jaxpr/sub | solution.py:25
  161.7 4.9 %fusion.89 = bf16[1,512,2,128]{3,1,2,0:T(8,128)(2,1)S(1)} fusion(bf16[2048,2,128]{2,0,1:T(8,128)(2,1)} %get-tuple-element.162, f32[2,512,2048]{2,1,0:T(8,128)} %get-tuple-element.138, f32[2,512]{1,0:T(2,128)S(1)} %get-tuple-element.139), kind=kOutput, calls=%fused_computation.10.clone.1 | convolution fusion | flops 541196288 | bytes 9703424 | tf_op jit(solution)/shard_map/while/body/eval_jaxpr/hqk,khd->qhd/dot_general | solution.py:27
  166.6 1.0 copy_dynamic-update-slice_fusion.2
  167.6 0.6 broadcast_compare_fusion.2
  168.2 7.7 %fusion.88 = (f32[2,512]{1,0:T(2,128)S(1)}, f32[2,512,2048]{2,1,0:T(8,128)}) fusion(pred[512,2048]{1,0:T(8,128)(4,1)S(1)} %broadcast_compare_fusion.2, bf16[2048,2,128]{2,0,1:T(8,128)(2,1)} %get-tuple-element.161, bf16[4,512,2,128]{3,1,0,2:T(8,128)(2,1)} %get-tuple-element.160, s32[]{:T(128)} %get-tuple-element.148), kind=kOutput, calls=%fused_computation.88.clone.1 | convolution fusion | flops 545261568 | bytes 10752512 | tf_op jit(solution)/shard_map/while/body/eval_jaxpr/sub | solution.py:25
  175.9 4.9 %fusion.89 = bf16[1,512,2,128]{3,1,2,0:T(8,128)(2,1)S(1)} fusion(bf16[2048,2,128]{2,0,1:T(8,128)(2,1)} %get-tuple-element.162, f32[2,512,2048]{2,1,0:T(8,128)} %get-tuple-element.138, f32[2,512]{1,0:T(2,128)S(1)} %get-tuple-element.139), kind=kOutput, calls=%fused_computation.10.clone.1 | convolution fusion | flops 541196288 | bytes 9703424 | tf_op jit(solution)/shard_map/while/body/eval_jaxpr/hqk,khd->qhd/dot_general | solution.py:27
  180.8 1.0 copy_dynamic-update-slice_fusion.2
  181.8 0.6 broadcast_compare_fusion.2
  182.4 7.7 %fusion.88 = (f32[2,512]{1,0:T(2,128)S(1)}, f32[2,512,2048]{2,1,0:T(8,128)}) fusion(pred[512,2048]{1,0:T(8,128)(4,1)S(1)} %broadcast_compare_fusion.2, bf16[2048,2,128]{2,0,1:T(8,128)(2,1)} %get-tuple-element.161, bf16[4,512,2,128]{3,1,0,2:T(8,128)(2,1)} %get-tuple-element.160, s32[]{:T(128)} %get-tuple-element.148), kind=kOutput, calls=%fused_computation.88.clone.1 | convolution fusion | flops 545261568 | bytes 10752512 | tf_op jit(solution)/shard_map/while/body/eval_jaxpr/sub | solution.py:25
  190.1 4.9 %fusion.89 = bf16[1,512,2,128]{3,1,2,0:T(8,128)(2,1)S(1)} fusion(bf16[2048,2,128]{2,0,1:T(8,128)(2,1)} %get-tuple-element.162, f32[2,512,2048]{2,1,0:T(8,128)} %get-tuple-element.138, f32[2,512]{1,0:T(2,128)S(1)} %get-tuple-element.139), kind=kOutput, calls=%fused_computation.10.clone.1 | convolution fusion | flops 541196288 | bytes 9703424 | tf_op jit(solution)/shard_map/while/body/eval_jaxpr/hqk,khd->qhd/dot_general | solution.py:27
  195.0 1.0 copy_dynamic-update-slice_fusion.2
  196.0 9.6 %convolution_convert_fusion = bf16[2048,3200]{1,0:T(8,128)(2,1)} fusion(bf16[256,3200]{1,0:T(8,128)(2,1)S(1)} %copy-done, bf16[256,8,2,128]{3,2,1,0:T(2,128)(2,1)} %bitcast.89), kind=kOutput, calls=%fused_computation.24 | convolution fusion | flops 3361996800 | bytes 15794176 | tf_op jit(solution)/shard_map/dot_general | solution.py:90
  205.6 0.3 reduce-scatter.5.cloned.1.call-start
  205.9 0.5 copy-done.5
  206.4 0.1 add.72
  206.5 0.1 mul.150
  206.6 75.4 %reduce-scatter.3.cloned.1.call-done = bf16[256,3200]{1,0:T(8,128)(2,1)} async-done(((bf16[2048,3200]{1,0:T(8,128)(2,1)}), bf16[256,3200]{1,0:T(8,128)(2,1)}) %reduce-scatter.3.cloned.1.call-update) | async-done | bytes 1638416 | tf_op jit(solution)/shard_map/reduce_scatter | solution.py:89
  282.1 3.5 convert_add_fusion
  285.6 5.2 %reshape.166 = f32[4,2,16,2,3200]{4,3,2,1,0:T(2,128)} reshape(f32[256,3200]{1,0:T(8,128)} %convert_add_fusion) | data formatting | bytes 6553600 | tf_op jit(solution)/shard_map/reshape | solution.py:99
  290.8 2.8 fusion.63
  293.6 0.1 copy-done.1
  293.7 1.9 multiply_reduce_fusion
  295.6 0.1 div.33
  295.7 4.0 copy.77
  299.7 0.1 rsqrt.29
  299.8 5.8 %reshape.167 = f32[64,16,800]{2,1,0:T(8,128)} reshape(f32[4,16,2,2,3200]{4,3,2,1,0:T(2,128)} %bitcast.85) | data formatting | bytes 6553600 | tf_op jit(solution)/shard_map/reshape | solution.py:99
  305.6 2.7 add_convert_fusion
  308.3 0.4 copy.46
  308.7 29.8 %all_to_all.26 = bf16[64,16,800]{2,0,1:T(8,128)(2,1)S(1)} all-to-all(bf16[64,16,800]{2,0,1:T(8,128)(2,1)S(1)} %copy.46), channel_id=1, replica_groups=mesh['rows'=16,'seq'=8] {'rows'}, dimensions={1} | all-to-all | bytes 3276800 | tf_op jit(solution)/shard_map/all_to_all | solution.py:114
  338.6 1.3 fusion.36
  339.8 0.4 copy.48
  340.3 19.6 %convolution_convert_fusion.1 = bf16[1024,6144]{1,0:T(8,128)(2,1)} fusion(bf16[1024,800]{1,0:T(8,128)(2,1)S(1)} %bitcast.88, bf16[800,6144]{1,0:T(8,128)(2,1)} %param.25), kind=kOutput, calls=%fused_computation.25 | convolution fusion | flops 10072621056 | bytes 24051712 | tf_op jit(solution)/shard_map/dot_general | solution.py:136
  359.9 0.7 copy-done.12
  360.6 0.2 reshape_squeeze.5
  360.7 0.1 slice_reduce_fusion
  360.8 0.1 convert_element_type.80
  360.9 0.6 broadcast_in_dim.28
  361.5 3.9 all-to-all-start.1
  365.4 6.3 %all-to-all-done.1 = bf16[64,16,1]{0,2,1:T(2,128)(2,1)S(1)} async-done(((bf16[64,16,1]{0,2,1:T(2,128)(2,1)}), bf16[64,16,1]{0,2,1:T(2,128)(2,1)S(1)}, u32[]{:S(2)}, u32[]{:S(2)}) %all-to-all-start.1) | async-done | bytes 2080 | tf_op jit(solution)/shard_map/all_to_all | solution.py:115
  371.7 0.1 fusion.56
  372.0 82.1 %reduce-scatter.5.cloned.1.call-done = bf16[64,6144]{1,0:T(8,128)(2,1)} async-done(((bf16[1024,6144]{1,0:T(8,128)(2,1)}), bf16[64,6144]{1,0:T(8,128)(2,1)}) %reduce-scatter.5.cloned.1.call-update) | async-done | bytes 786448 | tf_op jit(solution)/shard_map/reduce_scatter | solution.py:135
  454.1 5.2 %fusion.55 = bf16[1,64,6144]{2,1,0:T(8,128)(2,1)} fusion(bf16[64,6144]{1,0:T(8,128)(2,1)} %reduce-scatter.5.cloned.1.call-done, f32[64]{0:T(128)S(1)} %dynamic_slice.11, f32[6144]{0:T(1024)S(1)} %copy-done.7), kind=kLoop, calls=%fused_computation.72 | loop fusion | flops 26738688 | bytes 1597696 | tf_op jit(solution)/shard_map/broadcast_in_dim | solution.py:145
  (45 shorter events, 0.5 us)
Async XLA Ops:
  6.5 189.5 %copy-start = (bf16[256,3200]{1,0:T(8,128)(2,1)S(1)}, bf16[256,3200]{1,0:T(8,128)(2,1)}, u32[]{:S(2)}) copy-start(bf16[256,3200]{1,0:T(8,128)(2,1)} %param.19) | copy-start | bytes 4915204
  6.5 2.0 copy-start.3
  6.5 77.7 %all-gather.3.cloned.1.call-start = ((), (), s32[]{:S(2)}) async-start(), calls=%async_computation.4 | async-start | bytes 14745600 | tf_op jit(solution)/shard_map/all_gather | solution.py:62
  10.9 0.7 copy-start.11
  10.9 12.6 %copy-start.9 = (f32[2,256]{1,0:T(2,128)S(1)}, f32[2,256]{1,0:T(2,128)}, u32[]{:S(2)}) copy-start(f32[2,256]{1,0:T(2,128)} %param.18) | copy-start | bytes 6148
  11.0 271.1 %reduce-scatter.3.cloned.1.call-start = ((), (), s32[]{:S(2)}) async-start(), calls=%async_computation.5 | async-start | bytes 14745600 | tf_op jit(solution)/shard_map/reduce_scatter | solution.py:89
  134.6 3.2 copy-start.2
  205.6 0.8 copy-start.5
  205.6 0.9 copy-start.6
  205.6 76.4 %copy-start.4 = (bf16[1,256,3200]{2,1,0:T(8,128)(2,1)S(1)}, bf16[1,256,3200]{2,1,0:T(8,128)(2,1)}, u32[]{:S(2)}) copy-start(bf16[1,256,3200]{2,1,0:T(8,128)(2,1)} %param.15) | copy-start | bytes 4915204
  205.6 76.4 %copy-start.8 = (f32[3200]{0:T(1024)S(1)}, f32[3200]{0:T(1024)}, u32[]{:S(2)}) copy-start(f32[3200]{0:T(1024)} %param.20) | copy-start | bytes 38404
  205.6 248.5 %reduce-scatter.5.cloned.1.call-start = ((), (), s32[]{:S(2)}) async-start(), calls=%async_computation.6 | async-start | bytes 13369344 | tf_op jit(solution)/shard_map/reduce_scatter | solution.py:135
  290.8 2.9 copy-start.1
  308.7 29.9 %copy-start.10 = (s32[16]{0:T(128)S(1)}, s32[16]{0:T(128)}, u32[]{:S(2)}) copy-start(s32[16]{0:T(128)} %param.27) | copy-start | bytes 196
  359.9 0.7 copy-start.12
  359.9 94.2 %copy-start.7 = (f32[6144]{0:T(1024)S(1)}, f32[6144]{0:T(1024)}, u32[]{:S(2)}) copy-start(f32[6144]{0:T(1024)} %param.26) | copy-start | bytes 73732
  361.5 10.2 %all-to-all-start.1 = ((bf16[64,16,1]{0,2,1:T(2,128)(2,1)}), bf16[64,16,1]{0,2,1:T(2,128)(2,1)S(1)}, u32[]{:S(2)}, u32[]{:S(2)}) async-start(bf16[64,16,1]{0,2,1:T(2,128)(2,1)} %broadcast_in_dim.28), calls=%async_computation.3 | async-start | bytes 16384 | tf_op jit(solution)/shard_map/all_to_all | solution.py:115
Sparse Core Ops, SparseCore 0:
  11.1 73.1 all-gather.2
  205.8 76.2 reduce-scatter.2
  360.0 94.0 reduce-scatter.4
where the time goes:
time: 467 us; the launch traced here: 466 us
  waiting for transfers between devices  225 us (48%)
  matrix products  96.6 us (21%)
  blocking collectives  62.7 us (13%)
  local copies, waits for them, and re-layouts  33 us (7%)
  other arithmetic  31.5 us (7%)
  between operations  13.2 us (3%)
    reduce_scatter x1, waiting for transfers between devices, per_device(): lax.psum_scatter(jnp.dot(piece, fc_weight, preferred_element_type=jnp.flo...  82.1 us
    reduce_scatter x1, waiting for transfers between devices, per_device(): lax.psum_scatter(jnp.dot(piece, out_weight, preferred_element_type=jnp.fl...  75.4 us
    all_gather x1, waiting for transfers between devices, per_device(): lax.all_gather(normed, 'seq', axis=0, tiled=True)  60.7 us
    sub x4, matrix products, one_block(): exp_terms = jnp.exp(scores - peak_val)  30.7 us
    all_to_all x1, blocking collectives, per_device(): lax.all_to_all(merged_norm, 'rows', split_axis=1, concat_axis=0, tiled=True)  29.8 us
    psum x1, blocking collectives, per_device(): lax.psum((jnp.sum(query_raw * query_raw, axis=(1, 2)), jnp.sum(key_raw *...  21 us
    dot_general x4, matrix products, one_block(): jnp.einsum('hqk,khd->qhd', probs, value_half, preferred_element_type=jnp....  19.6 us
    dot_general x1, matrix products, per_device(): jnp.dot(piece, fc_weight, preferred_element_type=jnp.float32)  19.6 us
  transfers between devices with their start and end apart: 4, of which 4 were waited for; matrix products, arithmetic and copies ran while one was open for 0% of the time, Pallas kernels for 0%

commit v1 on v0

--- a/solution.py
+++ b/solution.py
@@ -7,6 +7,7 @@
 HEAD_DIM = 128
 HEADS = 16
 GRID = 32
+MASK_SHIFT = 1e6
 
 
 def attend_dense(query_norm, key_norm, value_half, row_segments, block_len, scale):
@@ -53,15 +54,14 @@
     fc_bias,
     owner,
 ):
+    seq_count = lax.axis_size("seq")
+    seq_me = lax.axis_index("seq")
     tokens = residual_in[0].astype(jnp.float32)
     shard_rows = tokens.shape[0]
     normed = (
         tokens * lax.rsqrt(jnp.mean(tokens * tokens, axis=-1, keepdims=True) + 1e-06) * norm_gain
     ).astype(jnp.bfloat16)
-    row_tokens, row_segments = (
-        lax.all_gather(normed, "seq", axis=0, tiled=True),
-        lax.all_gather(segment_ids[0].astype(jnp.bfloat16), "seq", axis=0, tiled=True),
-    )
+    row_tokens = lax.all_gather(normed, "seq", axis=0, tiled=True)
     length = row_tokens.shape[0]
     heads_here = qkv_weight.shape[1] // (3 * HEAD_DIM)
     projected = jnp.dot(row_tokens, qkv_weight, preferred_element_type=jnp.float32).reshape(
@@ -70,10 +70,23 @@
     query_raw = projected[:, :, 0]
     key_raw = projected[:, :, 1]
     value_half = projected[:, :, 2].astype(jnp.bfloat16)
-    query_sq, key_sq = lax.psum(
-        (jnp.sum(query_raw * query_raw, axis=(1, 2)), jnp.sum(key_raw * key_raw, axis=(1, 2))),
+    seg_spread = lax.dynamic_update_slice_in_dim(
+        jnp.zeros((length,), jnp.float32),
+        segment_ids[0].astype(jnp.float32),
+        seq_me * shard_rows,
+        0,
+    )
+    stats = lax.psum(
+        jnp.stack(
+            [
+                jnp.sum(query_raw * query_raw, axis=(1, 2)),
+                jnp.sum(key_raw * key_raw, axis=(1, 2)),
+                seg_spread,
+            ]
+        ),
         "seq",
     )
+    query_sq, key_sq, row_segments = stats[0], stats[1], stats[2]
     norm_width = HEADS * HEAD_DIM
     gain_pair = qk_gain.reshape(2, heads_here, HEAD_DIM)
     query_norm = (
@@ -85,13 +98,15 @@
     block_len = min(512, length)
     scale = HEAD_DIM ** (-0.5)
     attended = attend_dense(query_norm, key_norm, value_half, row_segments, block_len, scale)
-    piece = attended
-    attn = lax.psum_scatter(
-        jnp.dot(piece, out_weight, preferred_element_type=jnp.float32).astype(jnp.bfloat16),
-        "seq",
-        scatter_dimension=0,
-        tiled=True,
-    ).astype(jnp.float32)
+    group_width = attended.shape[1]
+    own_heads = lax.all_to_all(
+        attended.reshape(seq_count, shard_rows, group_width), "seq", 0, 0
+    )
+    full_out_weight = lax.all_gather(out_weight, "seq", axis=0, tiled=False)
+    group_terms = jnp.einsum(
+        "gtc,gcd->gtd", own_heads, full_out_weight, preferred_element_type=jnp.float32
+    ).astype(jnp.bfloat16)
+    attn = jnp.sum(group_terms.astype(jnp.float32), axis=0)
     hidden = tokens + layer_scale * attn
     half_grid = GRID // 2
     lines = shard_rows // (2 * GRID)
@@ -106,14 +121,11 @@
         pad_mask[0]
         .reshape(lines, 2, half_grid, 2)[:, 0, :, 0]
         .reshape(merged_count)
-        .astype(jnp.bfloat16)
+        .astype(jnp.float32)
     )
     row_count = lax.axis_size("rows")
-    mask_spread = jnp.broadcast_to(merged_mask[:, None], (merged_count, row_count))
-    slabs, slab_mask = (
-        lax.all_to_all(merged_norm, "rows", split_axis=1, concat_axis=0, tiled=True),
-        lax.all_to_all(mask_spread, "rows", split_axis=1, concat_axis=0, tiled=True),
-    )
+    row_me = lax.axis_index("rows")
+    slabs = lax.all_to_all(merged_norm, "rows", split_axis=1, concat_axis=0, tiled=True)
     owner_hot = (owner[None, :] == jnp.arange(row_count, dtype=jnp.int32)[:, None]).astype(
         jnp.bfloat16
     )
@@ -124,24 +136,19 @@
         preferred_element_type=jnp.float32,
     ).astype(jnp.bfloat16)
     ordered = ordered.reshape(row_count * merged_count, -1)
-    ordered_mask = jnp.einsum(
-        "jp,pms->jms",
-        owner_hot,
-        slab_mask.reshape(row_count, merged_count, 1),
-        preferred_element_type=jnp.float32,
+    partial = jnp.dot(ordered, fc_weight, preferred_element_type=jnp.float32).reshape(
+        row_count, merged_count, -1
     )
-    ordered_mask = ordered_mask.reshape(row_count * merged_count)
-    piece = ordered
+    own_slot = (jnp.arange(row_count, dtype=jnp.int32) == owner[row_me]).astype(jnp.float32)
+    shift = own_slot[:, None] * ((merged_mask - 1.0) * MASK_SHIFT)[None, :]
+    partial = (partial + shift[:, :, None]).astype(jnp.bfloat16)
     summed = lax.psum_scatter(
-        jnp.dot(piece, fc_weight, preferred_element_type=jnp.float32).astype(jnp.bfloat16),
+        partial.reshape(row_count * merged_count, -1),
         "rows",
         scatter_dimension=0,
         tiled=True,
     ).astype(jnp.float32)
-    own_mask = lax.dynamic_slice_in_dim(
-        ordered_mask, lax.axis_index("rows") * merged_count, merged_count, 0
-    )
-    result = jax.nn.gelu(summed + fc_bias, approximate=False) * own_mask[:, None]
+    result = jax.nn.gelu(summed + fc_bias, approximate=False)
     return result.astype(jnp.bfloat16)[None]
 
 

time: 467 us -> 405 us (0.87)
  blocking collectives: 62.7 us -> 22.6 us
  waiting for transfers between devices: 225 us -> 201 us
  starting transfers between devices: 4.18 us -> 14.9 us
    reduce_scatter x2 -> x1, waiting for transfers between devices: 158 us -> 95.1 us  [per_device(): lax.psum_scatter(partial.reshape(row_count * merged_count, -1), 'rows', s...]
    all_to_all x1 -> x0, blocking collectives: 29.8 us -> none  [per_device(): lax.all_to_all(merged_norm, 'rows', split_axis=1, concat_axis=0, tiled=True)]
    all_to_all x1 -> x2, waiting for transfers between devices: 6.33 us -> 32.2 us  [the longest x1 20.2 us: per_device(): lax.all_to_all(merged_norm, 'rows', split_axis=1, concat_axis=0, tiled=True)]
    all_gather x1 -> x0, blocking collectives: 11.9 us -> none  [per_device(): lax.all_gather(segment_ids[0].astype(jnp.bfloat16), 'seq', axis=0, tiled=...]
    all_gather x1 -> x2, waiting for transfers between devices: 60.7 us -> 72.5 us  [the longest x1 72.5 us: per_device(): row_tokens = lax.all_gather(normed, 'seq', axis=0, tiled=True)]
    all_to_all x1 -> x2, starting transfers between devices: 3.88 us -> 14.8 us  [the longest x1 7.77 us: per_device(): lax.all_to_all(attended.reshape(seq_count, shard_rows, group_width), 'seq...]
    reshape x4 -> x0, local copies, waits for them, and re-layouts: 9.26 us -> none  [the longest x2 9.17 us: per_device(): hidden.reshape(lines, 2, half_grid, 2, D)]
    reduce_sum x0 -> x1, local copies, waits for them, and re-layouts: none -> 5.33 us  [per_device(): attn = jnp.sum(group_terms.astype(jnp.float32), axis=0)]
  transfers between devices with their start and end apart: 4 -> 5, of which waited for: 4 -> 4; matrix products, arithmetic and copies ran while one was open for 0% -> 22% of each run, Pallas kernels for 0% -> 0%
where the time goes in v1:
time: 405 us
  waiting for transfers between devices  201 us (50%)
  matrix products  96.5 us (24%)
  local copies, waits for them, and re-layouts  29 us (7%)
  other arithmetic  27.6 us (7%)
  blocking collectives  22.6 us (6%)
  starting transfers between devices  14.9 us (4%)
  between operations  13.3 us (3%)
    reduce_scatter x1, waiting for transfers between devices, per_device(): lax.psum_scatter(partial.reshape(row_count * merged_count, -1), 'rows', s...  95.1 us
    all_gather x1, waiting for transfers between devices, per_device(): row_tokens = lax.all_gather(normed, 'seq', axis=0, tiled=True)  72.5 us
    sub x4, matrix products, one_block(): exp_terms = jnp.exp(scores - peak_val)  31 us
    psum x1, blocking collectives, per_device(): lax.psum(jnp.stack([jnp.sum(query_raw * query_raw, axis=(1, 2)), jnp.sum(...  22.6 us
    all_to_all x1, waiting for transfers between devices, per_device(): lax.all_to_all(merged_norm, 'rows', split_axis=1, concat_axis=0, tiled=True)  20.2 us
    dot_general x1, matrix products, per_device(): jnp.dot(ordered, fc_weight, preferred_element_type=jnp.float32)  19.2 us
    dot_general x4, matrix products, one_block(): jnp.einsum('hqk,khd->qhd', probs, value_half, preferred_element_type=jnp....  18.7 us
    dot_general x1, matrix products, per_device(): jnp.dot(row_tokens, qkv_weight, preferred_element_type=jnp.float32)  15.7 us
  transfers between devices with their start and end apart: 5, of which 4 were waited for; matrix products, arithmetic and copies ran while one was open for 22% of the time, Pallas kernels for 0%

profile of v1, /device:TPU:1, one launch (start us, length us, event | category | flops | bytes accessed | tf_op | source)
XLA Modules:
  0.0 404.6 jit_solution(10836090393352335551)
XLA Ops:
  6.5 2.0 fusion.28
  8.5 2.4 fusion.30
  11.0 0.7 all-gather.6.cloned.1.call-update
  11.7 72.5 %all-gather.4.cloned.1.call-done = bf16[2048,3200]{1,0:T(8,128)(2,1)} async-done(((bf16[256,3200]{1,0:T(8,128)(2,1)}), bf16[2048,3200]{1,0:T(8,128)(2,1)}) %all-gather.4.cloned.1.call-update) | async-done | bytes 13107216 | tf_op jit(solution)/shard_map/all_gather | solution.py:64
  84.2 15.7 %fusion.74 = f32[2048,768]{0,1:T(8,128)S(1)} fusion(bf16[2048,3200]{1,0:T(8,128)(2,1)} %all-gather.4.cloned.1.call-done, bf16[3200,768]{1,0:T(8,128)(2,1)} %param.17), kind=kOutput, calls=%fused_computation.97 | convolution fusion | flops 10066329600 | bytes 24313856 | tf_op jit(solution)/shard_map/dot_general | solution.py:67
  99.9 0.1 slice.44
  100.1 2.5 fusion.72
  102.5 1.9 copy.44
  104.4 2.9 copy.43
  107.3 0.3 fusion.31
  107.7 1.3 copy-done
  108.9 0.3 multiply_reduce_fusion.1
  109.3 22.6 %psum.7 = f32[3,2048]{1,0:T(4,128)S(1)} all-reduce(f32[3,2048]{1,0:T(4,128)S(1)} %pad_maximum_fusion), channel_id=1, replica_groups=mesh['rows'=16,'seq'=8] {'seq'}, use_global_device_ids=true, to_apply=%region_3.0 | all-reduce | flops 6144 | bytes 49152 | tf_op jit(solution)/shard_map/psum | solution.py:79
  131.9 0.1 fusion.62
  132.0 1.3 copy.45
  133.3 3.0 multiply_convert_fusion
  136.3 1.3 fusion.33
  137.6 53.7 %while.10 = (s32[]{:T(128)}, bf16[4,512,2,128]{3,2,1,0:T(2,128)(2,1)S(1)}, f32[4,512]{1,0:T(4,128)S(1)}, f32[1,2048]{1,0:T(1,128)S(1)}, bf16[4,512,2,128]{3,1,0,...) while((s32[]{:T(128)}, ...), condition=%wide.region_7.8_spmd, body=%wide.region_4.7_spmd.sunk | while | flops 1087506432 | bytes 26237560 | solution.py:32
  137.6 0.7 broadcast_compare_fusion.2
  138.3 7.8 %fusion.90 = (f32[2,512]{1,0:T(2,128)S(1)}, f32[2,512,2048]{2,1,0:T(8,128)}) fusion(pred[512,2048]{1,0:T(8,128)(4,1)S(1)} %broadcast_compare_fusion.2, bf16[2048,2,128]{2,0,1:T(8,128)(2,1)} %get-tuple-element.158, bf16[4,512,2,128]{3,1,0,2:T(8,128)(2,1)} %get-tuple-element.157, s32[]{:T(128)} %get-tuple-element.145), kind=kOutput, calls=%fused_computation.94.clone.1 | convolution fusion | flops 545261568 | bytes 10752512 | tf_op jit(solution)/shard_map/while/body/eval_jaxpr/sub | solution.py:26
  146.1 4.7 %fusion.91 = bf16[1,512,2,128]{3,1,2,0:T(8,128)(2,1)S(1)} fusion(bf16[2048,2,128]{2,0,1:T(8,128)(2,1)S(1)} %copy-done.5, f32[2,512,2048]{2,1,0:T(8,128)} %get-tuple-element.135, f32[2,512]{1,0:T(2,128)S(1)} %get-tuple-element.136), kind=kOutput, calls=%fused_computation.11.clone.1 | convolution fusion | flops 541196288 | bytes 9703424 | tf_op jit(solution)/shard_map/while/body/eval_jaxpr/hqk,khd->qhd/dot_general | solution.py:28
  150.8 0.3 copy_dynamic-update-slice_fusion.2
  151.1 0.7 broadcast_compare_fusion.2
  151.8 7.7 %fusion.90 = (f32[2,512]{1,0:T(2,128)S(1)}, f32[2,512,2048]{2,1,0:T(8,128)}) fusion(pred[512,2048]{1,0:T(8,128)(4,1)S(1)} %broadcast_compare_fusion.2, bf16[2048,2,128]{2,0,1:T(8,128)(2,1)} %get-tuple-element.158, bf16[4,512,2,128]{3,1,0,2:T(8,128)(2,1)} %get-tuple-element.157, s32[]{:T(128)} %get-tuple-element.145), kind=kOutput, calls=%fused_computation.94.clone.1 | convolution fusion | flops 545261568 | bytes 10752512 | tf_op jit(solution)/shard_map/while/body/eval_jaxpr/sub | solution.py:26
  159.5 4.7 %fusion.91 = bf16[1,512,2,128]{3,1,2,0:T(8,128)(2,1)S(1)} fusion(bf16[2048,2,128]{2,0,1:T(8,128)(2,1)S(1)} %copy-done.5, f32[2,512,2048]{2,1,0:T(8,128)} %get-tuple-element.135, f32[2,512]{1,0:T(2,128)S(1)} %get-tuple-element.136), kind=kOutput, calls=%fused_computation.11.clone.1 | convolution fusion | flops 541196288 | bytes 9703424 | tf_op jit(solution)/shard_map/while/body/eval_jaxpr/hqk,khd->qhd/dot_general | solution.py:28
  164.2 0.3 copy_dynamic-update-slice_fusion.2
  164.5 0.7 broadcast_compare_fusion.2
  165.2 7.7 %fusion.90 = (f32[2,512]{1,0:T(2,128)S(1)}, f32[2,512,2048]{2,1,0:T(8,128)}) fusion(pred[512,2048]{1,0:T(8,128)(4,1)S(1)} %broadcast_compare_fusion.2, bf16[2048,2,128]{2,0,1:T(8,128)(2,1)} %get-tuple-element.158, bf16[4,512,2,128]{3,1,0,2:T(8,128)(2,1)} %get-tuple-element.157, s32[]{:T(128)} %get-tuple-element.145), kind=kOutput, calls=%fused_computation.94.clone.1 | convolution fusion | flops 545261568 | bytes 10752512 | tf_op jit(solution)/shard_map/while/body/eval_jaxpr/sub | solution.py:26
  172.9 4.7 %fusion.91 = bf16[1,512,2,128]{3,1,2,0:T(8,128)(2,1)S(1)} fusion(bf16[2048,2,128]{2,0,1:T(8,128)(2,1)S(1)} %copy-done.5, f32[2,512,2048]{2,1,0:T(8,128)} %get-tuple-element.135, f32[2,512]{1,0:T(2,128)S(1)} %get-tuple-element.136), kind=kOutput, calls=%fused_computation.11.clone.1 | convolution fusion | flops 541196288 | bytes 9703424 | tf_op jit(solution)/shard_map/while/body/eval_jaxpr/hqk,khd->qhd/dot_general | solution.py:28
  177.6 0.3 copy_dynamic-update-slice_fusion.2
  177.9 0.7 broadcast_compare_fusion.2
  178.6 7.7 %fusion.90 = (f32[2,512]{1,0:T(2,128)S(1)}, f32[2,512,2048]{2,1,0:T(8,128)}) fusion(pred[512,2048]{1,0:T(8,128)(4,1)S(1)} %broadcast_compare_fusion.2, bf16[2048,2,128]{2,0,1:T(8,128)(2,1)} %get-tuple-element.158, bf16[4,512,2,128]{3,1,0,2:T(8,128)(2,1)} %get-tuple-element.157, s32[]{:T(128)} %get-tuple-element.145), kind=kOutput, calls=%fused_computation.94.clone.1 | convolution fusion | flops 545261568 | bytes 10752512 | tf_op jit(solution)/shard_map/while/body/eval_jaxpr/sub | solution.py:26
  186.3 4.7 %fusion.91 = bf16[1,512,2,128]{3,1,2,0:T(8,128)(2,1)S(1)} fusion(bf16[2048,2,128]{2,0,1:T(8,128)(2,1)S(1)} %copy-done.5, f32[2,512,2048]{2,1,0:T(8,128)} %get-tuple-element.135, f32[2,512]{1,0:T(2,128)S(1)} %get-tuple-element.136), kind=kOutput, calls=%fused_computation.11.clone.1 | convolution fusion | flops 541196288 | bytes 9703424 | tf_op jit(solution)/shard_map/while/body/eval_jaxpr/hqk,khd->qhd/dot_general | solution.py:28
  191.0 0.3 copy_dynamic-update-slice_fusion.2
  191.3 1.5 reshape_reshape.3
  192.8 7.8 %all-to-all-start = ((bf16[8,256,256]{2,1,0:T(8,128)(2,1)}), bf16[8,256,256]{2,1,0:T(8,128)(2,1)S(1)}, u32[]{:S(2)}, u32[]{:S(2)}) async-start(bf16[8,256,256]{2,1,0:T(8,128)(2,1)} %reshape_reshape.3), calls=%async_computation | async-start | bytes 2097152 | tf_op jit(solution)/shard_map/all_to_all | solution.py:102
  200.6 2.8 reshape.214
  203.4 0.1 add.97
  203.5 0.1 mul.171
  203.7 12.1 %all-to-all-done = bf16[8,256,256]{2,1,0:T(8,128)(2,1)S(1)} async-done(((bf16[8,256,256]{2,1,0:T(8,128)(2,1)}), bf16[8,256,256]{2,1,0:T(8,128)(2,1)S(1)}, u32[]{:S(2)}, u32[]{:S(2)}) %all-to-all-start) | async-done | bytes 1048608 | tf_op jit(solution)/shard_map/all_to_all | solution.py:102
  215.7 10.6 %convert_reduce_fusion = f32[256,3200]{1,0:T(8,128)} fusion(bf16[8,256,256]{2,1,0:T(8,128)(2,1)S(1)} %all-to-all-done, bf16[8,256,3200]{2,1,0:T(8,128)(2,1)} %bitcast.99), kind=kOutput, calls=%fused_computation.24 | convolution fusion | flops 3374284800 | bytes 17432576 | tf_op jit(solution)/shard_map/gtc,gcd->gtd/dot_general | solution.py:106
  226.3 5.3 %reduce_sum.69 = f32[4,2,16,2,3200]{4,3,2,1,0:T(2,128)} reshape(f32[256,3200]{1,0:T(8,128)} %convert_reduce_fusion) | data formatting | bytes 6553600 | tf_op jit(solution)/shard_map/reduce_sum | solution.py:109
  231.7 4.2 %fusion.66 = (f32[4,16]{1,0:T(4,128)S(1)}, f32[4,16,2,2,3200]{4,3,1,2,0:T(2,128)S(1)}) fusion(f32[4,2,16,2,3200]{4,3,2,1,0:T(2,128)S(1)} %copy-done.3, f32[4,2,16,2,3200]{4,3,2,1,0:T(2,128)} %reduce_sum.69, f32[3200]{0:T(1024)S(1)} %copy-done.9), kind=kLoop, calls=%fused_computation.93 | loop fusion | flops 2457536 | bytes 9843456 | tf_op jit(solution)/shard_map/reduce_sum | solution.py:117
  235.9 0.3 copy.36
  236.2 1.9 multiply_reduce_fusion
  238.1 0.1 div.33
  238.2 0.1 rsqrt.45
  238.3 4.5 %reshape.212 = f32[64,16,800]{2,1,0:T(8,128)} reshape(f32[4,16,2,2,3200]{4,3,2,1,0:T(2,128)S(1)} %copy.36) | data formatting | bytes 6553600 | tf_op jit(solution)/shard_map/reshape | solution.py:114
  242.7 2.7 add_convert_fusion.1
  245.5 1.7 copy.37
  247.1 7.0 %all-to-all-start.1 = ((bf16[64,16,800]{2,0,1:T(8,128)(2,1)}), bf16[64,16,800]{2,0,1:T(8,128)(2,1)S(1)}, u32[]{:S(2)}, u32[]{:S(2)}) async-start(bf16[64,16,800]{2,0,1:T(8,128)(2,1)} %copy.37), calls=%async_computation.1 | async-start | bytes 3670016 | tf_op jit(solution)/shard_map/all_to_all | solution.py:128
  254.2 0.5 broadcast.188
  254.7 0.7 reduce.16
  255.4 0.1 reshape_squeeze.8
  255.5 0.1 fusion.57
  255.6 0.1 mul.177
  255.7 0.6 dynamic_slice.11
  256.3 0.6 compare_convert_fusion
  257.0 0.1 broadcast_multiply_fusion
  257.0 20.2 %all-to-all-done.1 = bf16[64,16,800]{2,0,1:T(8,128)(2,1)S(1)} async-done(((bf16[64,16,800]{2,0,1:T(8,128)(2,1)}), bf16[64,16,800]{2,0,1:T(8,128)(2,1)S(1)}, u32[]{:S(2)}, u32[]{:S(2)}) %all-to-all-start.1) | async-done | bytes 1638432 | tf_op jit(solution)/shard_map/all_to_all | solution.py:128
  277.2 1.3 fusion.38
  278.5 19.2 %add_convert_fusion = bf16[16,64,6144]{2,1,0:T(8,128)(2,1)} fusion(f32[16,64]{1,0:T(8,128)S(1)} %broadcast_multiply_fusion, bf16[800,6144]{1,0:T(8,128)(2,1)} %param.25, bf16[16,64,800]{2,0,1:T(8,128)(2,1)S(1)} %fusion.38), kind=kOutput, calls=%fused_computation.25 | convolution fusion | flops 10078912512 | bytes 24055808 | tf_op jit(solution)/shard_map/dot_general | solution.py:139
  297.8 95.1 %reduce-scatter.2.cloned.1.call-done = bf16[64,6144]{1,0:T(8,128)(2,1)} async-done(((bf16[1024,6144]{1,0:T(8,128)(2,1)}), bf16[64,6144]{1,0:T(8,128)(2,1)}) %reduce-scatter.2.cloned.1.call-update) | async-done | bytes 786448 | tf_op jit(solution)/shard_map/reduce_scatter | solution.py:145
  392.9 5.2 %fusion.54 = bf16[1,64,6144]{2,1,0:T(8,128)(2,1)} fusion(bf16[64,6144]{1,0:T(8,128)(2,1)} %reduce-scatter.2.cloned.1.call-done, f32[6144]{0:T(1024)S(1)} %copy-done.8), kind=kLoop, calls=%fused_computation.70 | loop fusion | flops 26345472 | bytes 1597440 | tf_op jit(solution)/shard_map/broadcast_in_dim | solution.py:152
  (53 shorter events, 0.3 us)
Async XLA Ops:
  6.5 2.0 copy-start.1
  6.5 77.7 %all-gather.4.cloned.1.call-start = ((), (), s32[]{:S(2)}) async-start(), calls=%async_computation.3 | async-start | bytes 14745600 | tf_op jit(solution)/shard_map/all_gather | solution.py:64
  10.9 0.8 copy-start.11
  10.9 0.8 copy-start.10
  10.9 192.8 %all-gather.6.cloned.1.call-start = ((), (), s32[]{:S(2)}) async-start(), calls=%async_computation.5 | async-start | bytes 14745600 | tf_op jit(solution)/shard_map/all_gather | solution.py:105
  107.3 1.6 copy-start
  136.3 1.3 copy-start.4
  138.3 7.8 %copy-start.5 = (bf16[2048,2,128]{2,0,1:T(8,128)(2,1)S(1)}, bf16[2048,2,128]{2,0,1:T(8,128)(2,1)}, u32[]{:S(2)}) copy-start(bf16[2048,2,128]{2,0,1:T(8,128)(2,1)} %get-tuple-element.159) | copy-start | bytes 3145732 | tf_op jit(solution)/shard_map/while
  151.7 7.8 %copy-start.5 = (bf16[2048,2,128]{2,0,1:T(8,128)(2,1)S(1)}, bf16[2048,2,128]{2,0,1:T(8,128)(2,1)}, u32[]{:S(2)}) copy-start(bf16[2048,2,128]{2,0,1:T(8,128)(2,1)} %get-tuple-element.159) | copy-start | bytes 3145732 | tf_op jit(solution)/shard_map/while
  165.2 7.8 %copy-start.5 = (bf16[2048,2,128]{2,0,1:T(8,128)(2,1)S(1)}, bf16[2048,2,128]{2,0,1:T(8,128)(2,1)}, u32[]{:S(2)}) copy-start(bf16[2048,2,128]{2,0,1:T(8,128)(2,1)} %get-tuple-element.159) | copy-start | bytes 3145732 | tf_op jit(solution)/shard_map/while
  178.6 7.8 %copy-start.5 = (bf16[2048,2,128]{2,0,1:T(8,128)(2,1)S(1)}, bf16[2048,2,128]{2,0,1:T(8,128)(2,1)}, u32[]{:S(2)}) copy-start(bf16[2048,2,128]{2,0,1:T(8,128)(2,1)} %get-tuple-element.159) | copy-start | bytes 3145732 | tf_op jit(solution)/shard_map/while
  191.3 9.3 %copy-start.2 = (bf16[1,256,3200]{2,1,0:T(8,128)(2,1)S(1)}, bf16[1,256,3200]{2,1,0:T(8,128)(2,1)}, u32[]{:S(2)}) copy-start(bf16[1,256,3200]{2,1,0:T(8,128)(2,1)} %param.15) | copy-start | bytes 4915204
  192.8 22.9 %all-to-all-start = ((bf16[8,256,256]{2,1,0:T(8,128)(2,1)}), bf16[8,256,256]{2,1,0:T(8,128)(2,1)S(1)}, u32[]{:S(2)}, u32[]{:S(2)}) async-start(bf16[8,256,256]{2,1,0:T(8,128)(2,1)} %reshape_reshape.3), calls=%async_computation | async-start | bytes 2097152 | tf_op jit(solution)/shard_map/all_to_all | solution.py:102
  200.6 2.8 copy-start.6
  200.6 2.9 copy-start.7
  226.3 5.3 %copy-start.3 = (f32[4,2,16,2,3200]{4,3,2,1,0:T(2,128)S(1)}, f32[4,2,16,2,3200]{4,3,2,1,0:T(2,128)}, u32[]{:S(2)}) copy-start(f32[4,2,16,2,3200]{4,3,2,1,0:T(2,128)} %reshape.214) | copy-start | bytes 9830404
  226.3 5.3 %copy-start.9 = (f32[3200]{0:T(1024)S(1)}, f32[3200]{0:T(1024)}, u32[]{:S(2)}) copy-start(f32[3200]{0:T(1024)} %param.20) | copy-start | bytes 38404
  247.1 7.6 %copy-start.12 = (s32[1,256]{1,0:T(1,128)S(1)}, s32[1,256]{1,0:T(1,128)}, u32[]{:S(2)}) copy-start(s32[1,256]{1,0:T(1,128)} %param.22) | copy-start | bytes 3076
  247.1 8.6 %copy-start.13 = (s32[16]{0:T(128)S(1)}, s32[16]{0:T(128)}, u32[]{:S(2)}) copy-start(s32[16]{0:T(128)} %param.27) | copy-start | bytes 196
  247.1 30.1 %all-to-all-start.1 = ((bf16[64,16,800]{2,0,1:T(8,128)(2,1)}), bf16[64,16,800]{2,0,1:T(8,128)(2,1)S(1)}, u32[]{:S(2)}, u32[]{:S(2)}) async-start(bf16[64,16,800]{2,0,1:T(8,128)(2,1)} %copy.37), calls=%async_computation.1 | async-start | bytes 3670016 | tf_op jit(solution)/shard_map/all_to_all | solution.py:128
  254.2 138.7 %reduce-scatter.2.cloned.1.call-start = ((), (), s32[]{:S(2)}) async-start(), calls=%async_computation.4 | async-start | bytes 13369344 | tf_op jit(solution)/shard_map/reduce_scatter | solution.py:145
  297.7 95.1 %copy-start.8 = (f32[6144]{0:T(1024)S(1)}, f32[6144]{0:T(1024)}, u32[]{:S(2)}) copy-start(f32[6144]{0:T(1024)} %param.26) | copy-start | bytes 73732
Sparse Core Ops, SparseCore 0:
  11.0 73.1 all-gather.3
  85.9 70.2 all-gather.5
  297.9 94.9 reduce-scatter.1

commit v2 on v1

--- a/solution.py
+++ b/solution.py
@@ -1,13 +1,73 @@
 import jax
 import jax.numpy as jnp
 from jax import lax
+from jax.experimental import pallas as pl
+from jax.experimental.pallas import tpu as pltpu
 from jax.sharding import PartitionSpec as P
+
+MESH = pl.DeviceIdType.MESH
 
 D = 3200
 HEAD_DIM = 128
 HEADS = 16
 GRID = 32
 MASK_SHIFT = 1e6
+
+
+def seq_sum_kernel(part_ref, out_ref, slots, send_sem, recv_sem):
+    n = slots.shape[0]
+    me = lax.axis_index("seq")
+    row = lax.axis_index("rows")
+    barrier = pltpu.get_barrier_semaphore()
+    for k in range(1, n):
+        peer = lax.rem(me + k, n)
+        pl.semaphore_signal(barrier, inc=1, device_id=(row, peer), device_id_type=MESH)
+    pl.semaphore_wait(barrier, n - 1)
+    sends = []
+    for k in range(1, n):
+        peer = lax.rem(me + k, n)
+        copy = pltpu.make_async_remote_copy(
+            src_ref=part_ref,
+            dst_ref=slots.at[me],
+            send_sem=send_sem.at[k],
+            recv_sem=recv_sem.at[me],
+            device_id=(row, peer),
+            device_id_type=MESH,
+        )
+        copy.start()
+        sends.append(copy)
+    for k in range(1, n):
+        src = lax.rem(me + n - k, n)
+        pltpu.make_async_remote_copy(
+            src_ref=part_ref,
+            dst_ref=slots.at[src],
+            send_sem=send_sem.at[k],
+            recv_sem=recv_sem.at[src],
+            device_id=(row, src),
+            device_id_type=MESH,
+        ).wait_recv()
+    for copy in sends:
+        copy.wait_send()
+    total = jnp.zeros(out_ref.shape, jnp.float32)
+    for s in range(n):
+        total = total + jnp.where(s == me, part_ref[...], slots[s])
+    out_ref[...] = total
+
+
+def seq_sum(part):
+    n = lax.axis_size("seq")
+    return pl.pallas_call(
+        seq_sum_kernel,
+        out_shape=jax.ShapeDtypeStruct(part.shape, jnp.float32),
+        in_specs=[pl.BlockSpec(memory_space=pltpu.VMEM)],
+        out_specs=pl.BlockSpec(memory_space=pltpu.VMEM),
+        scratch_shapes=[
+            pltpu.VMEM((n,) + part.shape, jnp.float32),
+            pltpu.SemaphoreType.DMA((n,)),
+            pltpu.SemaphoreType.DMA((n,)),
+        ],
+        compiler_params=pltpu.CompilerParams(collective_id=0, has_side_effects=True),
+    )(part)
 
 
 def attend_dense(query_norm, key_norm, value_half, row_segments, block_len, scale):
@@ -76,15 +136,14 @@
         seq_me * shard_rows,
         0,
     )
-    stats = lax.psum(
+    stats = seq_sum(
         jnp.stack(
             [
                 jnp.sum(query_raw * query_raw, axis=(1, 2)),
                 jnp.sum(key_raw * key_raw, axis=(1, 2)),
                 seg_spread,
             ]
-        ),
-        "seq",
+        )
     )
     query_sq, key_sq, row_segments = stats[0], stats[1], stats[2]
     norm_width = HEADS * HEAD_DIM

time: 405 us -> 392 us (0.968)
  blocking collectives: 22.6 us -> 0 us
  Pallas kernels: 0 us -> 11.6 us
  starting transfers between devices: 14.9 us -> 10.7 us
    psum x1 -> x0, blocking collectives: 22.6 us -> none  [per_device(): lax.psum(jnp.stack([jnp.sum(query_raw * query_raw, axis=(1, 2)), jnp.sum(...]
    pallas_call x0 -> x1, Pallas kernels: none -> 11.6 us  [seq_sum(): pl.pallas_call(seq_sum_kernel, out_shape=jax.ShapeDtypeStruct(part.shape,...]
  transfers between devices with their start and end apart: 5 -> 5, of which waited for: 4 -> 4; matrix products, arithmetic and copies ran while one was open for 22% -> 24% of each run, Pallas kernels for 0% -> 3%
where the time goes in v2:
time: 392 us; the launch traced here: 391 us
  waiting for transfers between devices  200 us (51%)
  matrix products  96.6 us (25%)
  local copies, waits for them, and re-layouts  29 us (7%)
  other arithmetic  29 us (7%)
  between operations  13.3 us (3%)
  Pallas kernels  11.6 us (3%)
  starting transfers between devices  10.7 us (3%)
    reduce_scatter x1, waiting for transfers between devices, per_device(): lax.psum_scatter(partial.reshape(row_count * merged_count, -1), 'rows', s...  95.1 us
    all_gather x1, waiting for transfers between devices, per_device(): row_tokens = lax.all_gather(normed, 'seq', axis=0, tiled=True)  72.5 us
    sub x4, matrix products, one_block(): exp_terms = jnp.exp(scores - peak_val)  31 us
    all_to_all x1, waiting for transfers between devices, per_device(): lax.all_to_all(merged_norm, 'rows', split_axis=1, concat_axis=0, tiled=True)  20.2 us
    dot_general x1, matrix products, per_device(): jnp.dot(ordered, fc_weight, preferred_element_type=jnp.float32)  19.2 us
    dot_general x4, matrix products, one_block(): jnp.einsum('hqk,khd->qhd', probs, value_half, preferred_element_type=jnp....  18.9 us
    dot_general x1, matrix products, per_device(): jnp.dot(row_tokens, qkv_weight, preferred_element_type=jnp.float32)  15.7 us
    all_to_all x1, waiting for transfers between devices, per_device(): lax.all_to_all(attended.reshape(seq_count, shard_rows, group_width), 'seq...  12 us
  transfers between devices with their start and end apart: 5, of which 4 were waited for; matrix products, arithmetic and copies ran while one was open for 24% of the time, Pallas kernels for 3%

profile of v2, /device:TPU:1, one launch (start us, length us, event | category | flops | bytes accessed | tf_op | source)
XLA Modules:
  0.0 391.0 jit_solution(11638940976939539693)
XLA Ops:
  6.5 2.0 fusion.28
  8.5 2.4 fusion.30
  11.0 0.7 all-gather.6.cloned.1.call-update
  11.7 72.5 %all-gather.4.cloned.1.call-done = bf16[2048,3200]{1,0:T(8,128)(2,1)} async-done(((bf16[256,3200]{1,0:T(8,128)(2,1)}), bf16[2048,3200]{1,0:T(8,128)(2,1)}) %all-gather.4.cloned.1.call-update) | async-done | bytes 13107216 | tf_op jit(solution)/shard_map/all_gather | solution.py:124
  84.2 15.7 %fusion.69 = f32[2048,768]{0,1:T(8,128)S(1)} fusion(bf16[2048,3200]{1,0:T(8,128)(2,1)} %all-gather.4.cloned.1.call-done, bf16[3200,768]{1,0:T(8,128)(2,1)} %param.17), kind=kOutput, calls=%fused_computation.92 | convolution fusion | flops 10066329600 | bytes 24313856 | tf_op jit(solution)/shard_map/dot_general | solution.py:127
  99.9 0.1 slice.41
  100.1 2.5 fusion.67
  102.5 1.9 copy.44
  104.4 2.9 copy.43
  107.3 0.3 fusion.31
  107.7 1.3 copy-done
  108.9 0.3 multiply_reduce_fusion.1
  109.3 0.6 pad_maximum_fusion.part_ref
  109.9 11.6 %shard_map.127 = f32[3,2048]{1,0:T(4,128)} custom-call(f32[3,2048]{1,0:T(4,128)} %pad_maximum_fusion.part_ref), custom_call_target="tpu_custom_call" | custom-call | tf_op jit(solution)/shard_map/pallas_call | solution.py:59
  121.6 0.9 rsqrt_reduce_fusion
  122.5 1.3 copy.45
  123.9 3.0 multiply_convert_fusion
  126.8 1.3 fusion.33
  128.1 53.8 %while.10 = (s32[]{:T(128)}, bf16[4,512,2,128]{3,2,1,0:T(2,128)(2,1)S(1)}, f32[4,512]{1,0:T(4,128)S(1)}, f32[1,2048]{1,0:T(1,128)S(1)}, bf16[4,512,2,128]{3,1,0,...) while((s32[]{:T(128)}, ...), condition=%wide.region_6.7_spmd, body=%wide.region_3.6_spmd.sunk | while | flops 1087506432 | bytes 26237560 | solution.py:92
  128.1 0.7 broadcast_compare_fusion.2
  128.8 7.7 %fusion.85 = (f32[2,512]{1,0:T(2,128)S(1)}, f32[2,512,2048]{2,1,0:T(8,128)}) fusion(pred[512,2048]{1,0:T(8,128)(4,1)S(1)} %broadcast_compare_fusion.2, bf16[2048,2,128]{2,0,1:T(8,128)(2,1)} %get-tuple-element.158, bf16[4,512,2,128]{3,1,0,2:T(8,128)(2,1)} %get-tuple-element.157, s32[]{:T(128)} %get-tuple-element.145), kind=kOutput, calls=%fused_computation.89.clone.1 | convolution fusion | flops 545261568 | bytes 10752512 | tf_op jit(solution)/shard_map/while/body/eval_jaxpr/sub | solution.py:86
  136.5 4.7 %fusion.86 = bf16[1,512,2,128]{3,1,2,0:T(8,128)(2,1)S(1)} fusion(bf16[2048,2,128]{2,0,1:T(8,128)(2,1)S(1)} %copy-done.5, f32[2,512,2048]{2,1,0:T(8,128)} %get-tuple-element.135, f32[2,512]{1,0:T(2,128)S(1)} %get-tuple-element.136), kind=kOutput, calls=%fused_computation.11.clone.1 | convolution fusion | flops 541196288 | bytes 9703424 | tf_op jit(solution)/shard_map/while/body/eval_jaxpr/hqk,khd->qhd/dot_general | solution.py:88
  141.2 0.3 copy_dynamic-update-slice_fusion.2
  141.6 0.7 broadcast_compare_fusion.2
  142.2 7.7 %fusion.85 = (f32[2,512]{1,0:T(2,128)S(1)}, f32[2,512,2048]{2,1,0:T(8,128)}) fusion(pred[512,2048]{1,0:T(8,128)(4,1)S(1)} %broadcast_compare_fusion.2, bf16[2048,2,128]{2,0,1:T(8,128)(2,1)} %get-tuple-element.158, bf16[4,512,2,128]{3,1,0,2:T(8,128)(2,1)} %get-tuple-element.157, s32[]{:T(128)} %get-tuple-element.145), kind=kOutput, calls=%fused_computation.89.clone.1 | convolution fusion | flops 545261568 | bytes 10752512 | tf_op jit(solution)/shard_map/while/body/eval_jaxpr/sub | solution.py:86
  150.0 4.8 %fusion.86 = bf16[1,512,2,128]{3,1,2,0:T(8,128)(2,1)S(1)} fusion(bf16[2048,2,128]{2,0,1:T(8,128)(2,1)S(1)} %copy-done.5, f32[2,512,2048]{2,1,0:T(8,128)} %get-tuple-element.135, f32[2,512]{1,0:T(2,128)S(1)} %get-tuple-element.136), kind=kOutput, calls=%fused_computation.11.clone.1 | convolution fusion | flops 541196288 | bytes 9703424 | tf_op jit(solution)/shard_map/while/body/eval_jaxpr/hqk,khd->qhd/dot_general | solution.py:88
  154.8 0.3 copy_dynamic-update-slice_fusion.2
  155.1 0.7 broadcast_compare_fusion.2
  155.8 7.7 %fusion.85 = (f32[2,512]{1,0:T(2,128)S(1)}, f32[2,512,2048]{2,1,0:T(8,128)}) fusion(pred[512,2048]{1,0:T(8,128)(4,1)S(1)} %broadcast_compare_fusion.2, bf16[2048,2,128]{2,0,1:T(8,128)(2,1)} %get-tuple-element.158, bf16[4,512,2,128]{3,1,0,2:T(8,128)(2,1)} %get-tuple-element.157, s32[]{:T(128)} %get-tuple-element.145), kind=kOutput, calls=%fused_computation.89.clone.1 | convolution fusion | flops 545261568 | bytes 10752512 | tf_op jit(solution)/shard_map/while/body/eval_jaxpr/sub | solution.py:86
  163.5 4.7 %fusion.86 = bf16[1,512,2,128]{3,1,2,0:T(8,128)(2,1)S(1)} fusion(bf16[2048,2,128]{2,0,1:T(8,128)(2,1)S(1)} %copy-done.5, f32[2,512,2048]{2,1,0:T(8,128)} %get-tuple-element.135, f32[2,512]{1,0:T(2,128)S(1)} %get-tuple-element.136), kind=kOutput, calls=%fused_computation.11.clone.1 | convolution fusion | flops 541196288 | bytes 9703424 | tf_op jit(solution)/shard_map/while/body/eval_jaxpr/hqk,khd->qhd/dot_general | solution.py:88
  168.2 0.3 copy_dynamic-update-slice_fusion.2
  168.5 0.7 broadcast_compare_fusion.2
  169.2 7.7 %fusion.85 = (f32[2,512]{1,0:T(2,128)S(1)}, f32[2,512,2048]{2,1,0:T(8,128)}) fusion(pred[512,2048]{1,0:T(8,128)(4,1)S(1)} %broadcast_compare_fusion.2, bf16[2048,2,128]{2,0,1:T(8,128)(2,1)} %get-tuple-element.158, bf16[4,512,2,128]{3,1,0,2:T(8,128)(2,1)} %get-tuple-element.157, s32[]{:T(128)} %get-tuple-element.145), kind=kOutput, calls=%fused_computation.89.clone.1 | convolution fusion | flops 545261568 | bytes 10752512 | tf_op jit(solution)/shard_map/while/body/eval_jaxpr/sub | solution.py:86
  177.0 4.7 %fusion.86 = bf16[1,512,2,128]{3,1,2,0:T(8,128)(2,1)S(1)} fusion(bf16[2048,2,128]{2,0,1:T(8,128)(2,1)S(1)} %copy-done.5, f32[2,512,2048]{2,1,0:T(8,128)} %get-tuple-element.135, f32[2,512]{1,0:T(2,128)S(1)} %get-tuple-element.136), kind=kOutput, calls=%fused_computation.11.clone.1 | convolution fusion | flops 541196288 | bytes 9703424 | tf_op jit(solution)/shard_map/while/body/eval_jaxpr/hqk,khd->qhd/dot_general | solution.py:88
  181.6 0.3 copy_dynamic-update-slice_fusion.2
  182.0 1.5 reshape_reshape.3
  183.5 3.8 all-to-all-start
  187.3 2.8 reshape.214
  190.1 0.1 add.95
  190.2 0.1 mul.171
  190.3 12.0 %all-to-all-done = bf16[8,256,256]{2,1,0:T(8,128)(2,1)S(1)} async-done(((bf16[8,256,256]{2,1,0:T(8,128)(2,1)}), bf16[8,256,256]{2,1,0:T(8,128)(2,1)S(1)}, u32[]{:S(2)}, u32[]{:S(2)}) %all-to-all-start) | async-done | bytes 1048608 | tf_op jit(solution)/shard_map/all_to_all | solution.py:161
  202.3 10.6 %convert_reduce_fusion = f32[256,3200]{1,0:T(8,128)} fusion(bf16[8,256,256]{2,1,0:T(8,128)(2,1)S(1)} %all-to-all-done, bf16[8,256,3200]{2,1,0:T(8,128)(2,1)} %bitcast.99), kind=kOutput, calls=%fused_computation.24 | convolution fusion | flops 3374284800 | bytes 17432576 | tf_op jit(solution)/shard_map/gtc,gcd->gtd/dot_general | solution.py:165
  212.9 5.3 %reduce_sum.69 = f32[4,2,16,2,3200]{4,3,2,1,0:T(2,128)} reshape(f32[256,3200]{1,0:T(8,128)} %convert_reduce_fusion) | data formatting | bytes 6553600 | tf_op jit(solution)/shard_map/reduce_sum | solution.py:168
  218.3 4.2 %fusion.61 = (f32[4,16]{1,0:T(4,128)S(1)}, f32[4,16,2,2,3200]{4,3,1,2,0:T(2,128)S(1)}) fusion(f32[4,2,16,2,3200]{4,3,2,1,0:T(2,128)S(1)} %copy-done.3, f32[4,2,16,2,3200]{4,3,2,1,0:T(2,128)} %reduce_sum.69, f32[3200]{0:T(1024)S(1)} %copy-done.9), kind=kLoop, calls=%fused_computation.88 | loop fusion | flops 2457536 | bytes 9843456 | tf_op jit(solution)/shard_map/reduce_sum | solution.py:176
  222.5 0.3 copy.36
  222.8 1.9 multiply_reduce_fusion
  224.7 0.1 div.33
  224.8 0.1 rsqrt.45
  224.9 4.5 %reshape.212 = f32[64,16,800]{2,1,0:T(8,128)} reshape(f32[4,16,2,2,3200]{4,3,2,1,0:T(2,128)S(1)} %copy.36) | data formatting | bytes 6553600 | tf_op jit(solution)/shard_map/reshape | solution.py:173
  229.3 2.7 add_convert_fusion.1
  232.1 1.7 copy.37
  233.7 6.8 %all-to-all-start.1 = ((bf16[64,16,800]{2,0,1:T(8,128)(2,1)}), bf16[64,16,800]{2,0,1:T(8,128)(2,1)S(1)}, u32[]{:S(2)}, u32[]{:S(2)}) async-start(bf16[64,16,800]{2,0,1:T(8,128)(2,1)} %copy.37), calls=%async_computation.1 | async-start | bytes 3670016 | tf_op jit(solution)/shard_map/all_to_all | solution.py:187
  240.6 0.5 broadcast.188
  241.2 0.7 reduce.16
  241.8 0.1 reshape_squeeze.8
  242.0 0.1 fusion.57
  242.1 0.1 mul.177
  242.1 0.6 dynamic_slice.11
  242.7 0.6 compare_convert_fusion
  243.5 20.2 %all-to-all-done.1 = bf16[64,16,800]{2,0,1:T(8,128)(2,1)S(1)} async-done(((bf16[64,16,800]{2,0,1:T(8,128)(2,1)}), bf16[64,16,800]{2,0,1:T(8,128)(2,1)S(1)}, u32[]{:S(2)}, u32[]{:S(2)}) %all-to-all-start.1) | async-done | bytes 1638432 | tf_op jit(solution)/shard_map/all_to_all | solution.py:187
  263.6 1.3 fusion.38
  264.9 19.2 %add_convert_fusion = bf16[16,64,6144]{2,1,0:T(8,128)(2,1)} fusion(f32[16,64]{1,0:T(8,128)S(1)} %broadcast_multiply_fusion, bf16[800,6144]{1,0:T(8,128)(2,1)} %param.25, bf16[16,64,800]{2,0,1:T(8,128)(2,1)S(1)} %fusion.38), kind=kOutput, calls=%fused_computation.25 | convolution fusion | flops 10078912512 | bytes 24055808 | tf_op jit(solution)/shard_map/dot_general | solution.py:198
  284.2 95.1 %reduce-scatter.2.cloned.1.call-done = bf16[64,6144]{1,0:T(8,128)(2,1)} async-done(((bf16[1024,6144]{1,0:T(8,128)(2,1)}), bf16[64,6144]{1,0:T(8,128)(2,1)}) %reduce-scatter.2.cloned.1.call-update) | async-done | bytes 786448 | tf_op jit(solution)/shard_map/reduce_scatter | solution.py:204
  379.2 5.2 %fusion.54 = bf16[1,64,6144]{2,1,0:T(8,128)(2,1)} fusion(bf16[64,6144]{1,0:T(8,128)(2,1)} %reduce-scatter.2.cloned.1.call-done, f32[6144]{0:T(1024)S(1)} %copy-done.8), kind=kLoop, calls=%fused_computation.70 | loop fusion | flops 26345472 | bytes 1597440 | tf_op jit(solution)/shard_map/broadcast_in_dim | solution.py:211
  (53 shorter events, 0.4 us)
Async XLA Ops:
  6.5 2.0 copy-start.1
  6.5 77.7 %all-gather.4.cloned.1.call-start = ((), (), s32[]{:S(2)}) async-start(), calls=%async_computation.3 | async-start | bytes 14745600 | tf_op jit(solution)/shard_map/all_gather | solution.py:124
  10.9 0.8 copy-start.11
  10.9 0.8 copy-start.10
  10.9 179.4 %all-gather.6.cloned.1.call-start = ((), (), s32[]{:S(2)}) async-start(), calls=%async_computation.5 | async-start | bytes 14745600 | tf_op jit(solution)/shard_map/all_gather | solution.py:164
  107.3 1.6 copy-start
  126.8 1.3 copy-start.4
  128.8 7.7 %copy-start.5 = (bf16[2048,2,128]{2,0,1:T(8,128)(2,1)S(1)}, bf16[2048,2,128]{2,0,1:T(8,128)(2,1)}, u32[]{:S(2)}) copy-start(bf16[2048,2,128]{2,0,1:T(8,128)(2,1)} %get-tuple-element.159) | copy-start | bytes 3145732 | tf_op jit(solution)/shard_map/while
  142.2 7.8 %copy-start.5 = (bf16[2048,2,128]{2,0,1:T(8,128)(2,1)S(1)}, bf16[2048,2,128]{2,0,1:T(8,128)(2,1)}, u32[]{:S(2)}) copy-start(bf16[2048,2,128]{2,0,1:T(8,128)(2,1)} %get-tuple-element.159) | copy-start | bytes 3145732 | tf_op jit(solution)/shard_map/while
  155.8 7.8 %copy-start.5 = (bf16[2048,2,128]{2,0,1:T(8,128)(2,1)S(1)}, bf16[2048,2,128]{2,0,1:T(8,128)(2,1)}, u32[]{:S(2)}) copy-start(bf16[2048,2,128]{2,0,1:T(8,128)(2,1)} %get-tuple-element.159) | copy-start | bytes 3145732 | tf_op jit(solution)/shard_map/while
  169.2 7.8 %copy-start.5 = (bf16[2048,2,128]{2,0,1:T(8,128)(2,1)S(1)}, bf16[2048,2,128]{2,0,1:T(8,128)(2,1)}, u32[]{:S(2)}) copy-start(bf16[2048,2,128]{2,0,1:T(8,128)(2,1)} %get-tuple-element.159) | copy-start | bytes 3145732 | tf_op jit(solution)/shard_map/while
  181.9 5.3 %copy-start.2 = (bf16[1,256,3200]{2,1,0:T(8,128)(2,1)S(1)}, bf16[1,256,3200]{2,1,0:T(8,128)(2,1)}, u32[]{:S(2)}) copy-start(bf16[1,256,3200]{2,1,0:T(8,128)(2,1)} %param.15) | copy-start | bytes 4915204
  183.5 18.9 %all-to-all-start = ((bf16[8,256,256]{2,1,0:T(8,128)(2,1)}), bf16[8,256,256]{2,1,0:T(8,128)(2,1)S(1)}, u32[]{:S(2)}, u32[]{:S(2)}) async-start(bf16[8,256,256]{2,1,0:T(8,128)(2,1)} %reshape_reshape.3), calls=%async_computation | async-start | bytes 2097152 | tf_op jit(solution)/shard_map/all_to_all | solution.py:161
  187.3 2.8 copy-start.6
  187.3 2.9 copy-start.7
  212.9 5.3 %copy-start.3 = (f32[4,2,16,2,3200]{4,3,2,1,0:T(2,128)S(1)}, f32[4,2,16,2,3200]{4,3,2,1,0:T(2,128)}, u32[]{:S(2)}) copy-start(f32[4,2,16,2,3200]{4,3,2,1,0:T(2,128)} %reshape.214) | copy-start | bytes 9830404
  212.9 5.3 %copy-start.9 = (f32[3200]{0:T(1024)S(1)}, f32[3200]{0:T(1024)}, u32[]{:S(2)}) copy-start(f32[3200]{0:T(1024)} %param.20) | copy-start | bytes 38404
  233.7 7.4 %copy-start.12 = (s32[1,256]{1,0:T(1,128)S(1)}, s32[1,256]{1,0:T(1,128)}, u32[]{:S(2)}) copy-start(s32[1,256]{1,0:T(1,128)} %param.22) | copy-start | bytes 3076
  233.7 8.4 %copy-start.13 = (s32[16]{0:T(128)S(1)}, s32[16]{0:T(128)}, u32[]{:S(2)}) copy-start(s32[16]{0:T(128)} %param.27) | copy-start | bytes 196
  233.7 29.9 %all-to-all-start.1 = ((bf16[64,16,800]{2,0,1:T(8,128)(2,1)}), bf16[64,16,800]{2,0,1:T(8,128)(2,1)S(1)}, u32[]{:S(2)}, u32[]{:S(2)}) async-start(bf16[64,16,800]{2,0,1:T(8,128)(2,1)} %copy.37), calls=%async_computation.1 | async-start | bytes 3670016 | tf_op jit(solution)/shard_map/all_to_all | solution.py:187
  240.6 138.6 %reduce-scatter.2.cloned.1.call-start = ((), (), s32[]{:S(2)}) async-start(), calls=%async_computation.4 | async-start | bytes 13369344 | tf_op jit(solution)/shard_map/reduce_scatter | solution.py:204
  284.1 95.1 %copy-start.8 = (f32[6144]{0:T(1024)S(1)}, f32[6144]{0:T(1024)}, u32[]{:S(2)}) copy-start(f32[6144]{0:T(1024)} %param.26) | copy-start | bytes 73732
Sparse Core Ops, SparseCore 0:
  11.0 73.1 all-gather.3
  85.9 72.7 all-gather.5
  284.3 94.8 reduce-scatter.1

commit v3 on v2

--- a/solution.py
+++ b/solution.py
@@ -70,7 +70,7 @@
     )(part)
 
 
-def attend_dense(query_norm, key_norm, value_half, row_segments, block_len, scale):
+def attend_dense(query_norm, query_segments, key_norm, value_half, row_segments, block_len, scale):
     length, heads_here = (query_norm.shape[0], query_norm.shape[1])
     block_count = length // block_len
 
@@ -93,7 +93,7 @@
         one_block,
         (
             query_norm.reshape(block_count, block_len, heads_here, HEAD_DIM),
-            row_segments.reshape(block_count, block_len),
+            query_segments.reshape(block_count, block_len),
         ),
     )
     return blocks_out.reshape(length, heads_here * HEAD_DIM)
@@ -154,22 +154,66 @@
     key_norm = (
         key_raw * lax.rsqrt(key_sq / norm_width + 1e-06)[:, None, None] * gain_pair[1]
     ).astype(jnp.bfloat16)
-    block_len = min(512, length)
     scale = HEAD_DIM ** (-0.5)
-    attended = attend_dense(query_norm, key_norm, value_half, row_segments, block_len, scale)
-    group_width = attended.shape[1]
-    own_heads = lax.all_to_all(
-        attended.reshape(seq_count, shard_rows, group_width), "seq", 0, 0
-    )
     full_out_weight = lax.all_gather(out_weight, "seq", axis=0, tiled=False)
-    group_terms = jnp.einsum(
-        "gtc,gcd->gtd", own_heads, full_out_weight, preferred_element_type=jnp.float32
-    ).astype(jnp.bfloat16)
-    attn = jnp.sum(group_terms.astype(jnp.float32), axis=0)
-    hidden = tokens + layer_scale * attn
+    row_count = lax.axis_size("rows")
+    row_me = lax.axis_index("rows")
+    owner_hot = (owner[None, :] == jnp.arange(row_count, dtype=jnp.int32)[:, None]).astype(
+        jnp.bfloat16
+    )
+    own_slot = (jnp.arange(row_count, dtype=jnp.int32) == owner[row_me]).astype(jnp.float32)
+    parts = 2
+    part_rows = shard_rows // parts
+    query_parts = query_norm.reshape(seq_count, parts, part_rows, heads_here, HEAD_DIM)
+    seg_parts = row_segments.reshape(seq_count, parts, part_rows)
+    token_parts = tokens.reshape(parts, part_rows, D)
+    mask_parts = pad_mask[0].reshape(parts, part_rows)
+    results = []
+    next_queries = query_parts[:, 0]
+    for part in range(parts):
+        attended = attend_dense(
+            next_queries.reshape(seq_count * part_rows, heads_here, HEAD_DIM),
+            seg_parts[:, part].reshape(seq_count * part_rows),
+            key_norm,
+            value_half,
+            row_segments,
+            part_rows * 4,
+            scale,
+        )
+        group_width = attended.shape[1]
+        own_heads = lax.all_to_all(
+            attended.reshape(seq_count, part_rows, group_width), "seq", 0, 0
+        )
+        group_terms = jnp.einsum(
+            "gtc,gcd->gtd", own_heads, full_out_weight, preferred_element_type=jnp.float32
+        ).astype(jnp.bfloat16)
+        attn = jnp.sum(group_terms.astype(jnp.float32), axis=0)
+        partial = project_part(
+            token_parts[part] + layer_scale * attn,
+            mask_parts[part],
+            ln_weight,
+            ln_bias,
+            fc_weight,
+            owner_hot,
+            own_slot,
+        )
+        if part + 1 < parts:
+            partial, next_queries = lax.optimization_barrier((partial, query_parts[:, part + 1]))
+        summed = lax.psum_scatter(partial, "rows", scatter_dimension=0, tiled=True)
+        results.append(
+            jax.nn.gelu(summed.astype(jnp.float32) + fc_bias, approximate=False).astype(
+                jnp.bfloat16
+            )
+        )
+    return jnp.concatenate(results, axis=0)[None]
+
+
+def project_part(hidden, pad_mask, ln_weight, ln_bias, fc_weight, owner_hot, own_slot):
+    row_count = owner_hot.shape[0]
+    token_count = hidden.shape[0]
     half_grid = GRID // 2
-    lines = shard_rows // (2 * GRID)
-    merged_count = shard_rows // 4
+    lines = token_count // (2 * GRID)
+    merged_count = token_count // 4
     merged = jnp.transpose(hidden.reshape(lines, 2, half_grid, 2, D), (0, 2, 1, 3, 4)).reshape(
         merged_count, 4 * D
     )
@@ -177,17 +221,11 @@
     spread = jnp.mean(centre * centre, axis=-1, keepdims=True)
     merged_norm = (centre * lax.rsqrt(spread + 1e-05) * ln_weight + ln_bias).astype(jnp.bfloat16)
     merged_mask = (
-        pad_mask[0]
-        .reshape(lines, 2, half_grid, 2)[:, 0, :, 0]
+        pad_mask.reshape(lines, 2, half_grid, 2)[:, 0, :, 0]
         .reshape(merged_count)
         .astype(jnp.float32)
     )
-    row_count = lax.axis_size("rows")
-    row_me = lax.axis_index("rows")
     slabs = lax.all_to_all(merged_norm, "rows", split_axis=1, concat_axis=0, tiled=True)
-    owner_hot = (owner[None, :] == jnp.arange(row_count, dtype=jnp.int32)[:, None]).astype(
-        jnp.bfloat16
-    )
     ordered = jnp.einsum(
         "jp,pms->jms",
         owner_hot,
@@ -198,17 +236,9 @@
     partial = jnp.dot(ordered, fc_weight, preferred_element_type=jnp.float32).reshape(
         row_count, merged_count, -1
     )
-    own_slot = (jnp.arange(row_count, dtype=jnp.int32) == owner[row_me]).astype(jnp.float32)
     shift = own_slot[:, None] * ((merged_mask - 1.0) * MASK_SHIFT)[None, :]
     partial = (partial + shift[:, :, None]).astype(jnp.bfloat16)
-    summed = lax.psum_scatter(
-        partial.reshape(row_count * merged_count, -1),
-        "rows",
-        scatter_dimension=0,
-        tiled=True,
-    ).astype(jnp.float32)
-    result = jax.nn.gelu(summed + fc_bias, approximate=False)
-    return result.astype(jnp.bfloat16)[None]
+    return partial.reshape(row_count * merged_count, -1)
 
 
 def solution(mesh):

time: 392 us -> 430 us (1.097); the launches traced: 391 us -> 421 us
  waiting for transfers between devices: 200 us -> 173 us
  blocking collectives: 0 us -> 21.2 us
  local copies, waits for them, and re-layouts: 29 us -> 42.7 us
  matrix products: 96.6 us -> 106 us
  starting transfers between devices: 10.7 us -> 18.3 us
  other arithmetic: 29 us -> 33.7 us
    all_to_all x0 -> x1, blocking collectives: none -> 21.2 us  [project_part(): lax.all_to_all(merged_norm, 'rows', split_axis=1, concat_axis=0, tiled=True)]
    reduce_scatter x1 -> x2, waiting for transfers between devices: 95.1 us -> 78.9 us  [per_device(): summed = lax.psum_scatter(partial, 'rows', scatter_dimension=0, tiled=True)]
    all_to_all x2 -> x3, waiting for transfers between devices: 32.2 us -> 21.3 us  [the longest x2 11.2 us: per_device(): lax.all_to_all(attended.reshape(seq_count, part_rows, group_width), 'seq'...]
    all_to_all x2 -> x3, starting transfers between devices: 10.6 us -> 18 us  [the longest x2 11.3 us: per_device(): lax.all_to_all(attended.reshape(seq_count, part_rows, group_width), 'seq'...]
    squeeze x0 -> x2, local copies, waits for them, and re-layouts: none -> 5.25 us  [per_device(): token_parts[part] + layer_scale * attn]
    dot_general x2 -> x4, matrix products: 20.5 us -> 25.7 us  [the longest x2 24.9 us: project_part(): jnp.dot(ordered, fc_weight, preferred_element_type=jnp.float32)]
    dot_general x1 -> x2, matrix products: 10.6 us -> 14.1 us  [per_device(): jnp.einsum('gtc,gcd->gtd', own_heads, full_out_weight, preferred_element_...]
  transfers between devices with their start and end apart: 5 -> 7, of which waited for: 4 -> 5; matrix products, arithmetic and copies ran while one was open for 24% -> 32% of each run, Pallas kernels for 3% -> 3%
where the time goes in v3:
time: 430 us; the launch traced here: 421 us
  waiting for transfers between devices  173 us (40%)
  matrix products  106 us (25%)
  local copies, waits for them, and re-layouts  42.7 us (10%)
  other arithmetic  33.7 us (8%)
  blocking collectives  21.2 us (5%)
  starting transfers between devices  18.3 us (4%)
  between operations  14 us (3%)
  Pallas kernels  11.5 us (3%)
    reduce_scatter x2, waiting for transfers between devices, per_device(): summed = lax.psum_scatter(partial, 'rows', scatter_dimension=0, tiled=True)  78.9 us
    all_gather x1, waiting for transfers between devices, per_device(): row_tokens = lax.all_gather(normed, 'seq', axis=0, tiled=True)  72.5 us
    sub x4, matrix products, one_block(): exp_terms = jnp.exp(scores - peak_val)  30.7 us
    dot_general x2, matrix products, project_part(): jnp.dot(ordered, fc_weight, preferred_element_type=jnp.float32)  24.9 us
    all_to_all x1, blocking collectives, project_part(): lax.all_to_all(merged_norm, 'rows', split_axis=1, concat_axis=0, tiled=True)  21.2 us
    dot_general x4, matrix products, one_block(): jnp.einsum('hqk,khd->qhd', probs, value_half, preferred_element_type=jnp....  19.9 us
    dot_general x1, matrix products, per_device(): jnp.dot(row_tokens, qkv_weight, preferred_element_type=jnp.float32)  15.7 us
    dot_general x2, matrix products, per_device(): jnp.einsum('gtc,gcd->gtd', own_heads, full_out_weight, preferred_element_...  14.1 us
  transfers between devices with their start and end apart: 7, of which 5 were waited for; matrix products, arithmetic and copies ran while one was open for 32% of the time, Pallas kernels for 3%

profile of v3, /device:TPU:1, one launch (start us, length us, event | category | flops | bytes accessed | tf_op | source)
XLA Modules:
  0.0 421.5 jit_solution(14741189684142551469)
XLA Ops:
  6.5 2.0 fusion.62
  8.5 2.4 fusion.64
  11.0 0.7 all-gather.6.cloned.1.call-update
  11.7 72.5 %all-gather.4.cloned.1.call-done = bf16[2048,3200]{1,0:T(8,128)(2,1)} async-done(((bf16[256,3200]{1,0:T(8,128)(2,1)}), bf16[2048,3200]{1,0:T(8,128)(2,1)}) %all-gather.4.cloned.1.call-update) | async-done | bytes 13107216 | tf_op jit(solution)/shard_map/all_gather | solution.py:124
  84.2 15.7 %fusion.127 = f32[2048,768]{0,1:T(8,128)S(1)} fusion(bf16[2048,3200]{1,0:T(8,128)(2,1)} %all-gather.4.cloned.1.call-done, bf16[3200,768]{1,0:T(8,128)(2,1)} %param.19), kind=kOutput, calls=%fused_computation.167 | convolution fusion | flops 10066329600 | bytes 24313856 | tf_op jit(solution)/shard_map/dot_general | solution.py:127
  100.1 2.4 fusion.123
  102.5 2.9 copy.66
  105.4 3.1 copy.65
  108.4 2.1 fusion.65
  111.7 11.5 %shard_map.127 = f32[3,2048]{1,0:T(4,128)} custom-call(f32[3,2048]{1,0:T(4,128)} %pad_maximum_fusion.part_ref), custom_call_target="tpu_custom_call" | custom-call | tf_op jit(solution)/shard_map/pallas_call | solution.py:59
  123.1 0.9 add_rsqrt_fusion
  124.7 1.3 copy.67
  126.0 2.2 multiply_convert_fusion
  128.2 1.1 fusion.125
  129.2 1.3 fusion.67
  130.9 27.8 %while.20 = (s32[]{:T(128)}, bf16[2,512,2,128]{3,2,1,0:T(2,128)(2,1)S(1)}, f32[2,512]{1,0:T(2,128)S(1)}, f32[1,2048]{1,0:T(1,128)S(1)}, bf16[2,512,2,128]{3,1,0,...) while((s32[]{:T(128)}, ...), condition=%wide.region_6.7_spmd, body=%wide.region_3.6_spmd.sunk | while | flops 1087506432 | bytes 22042728 | solution.py:92
  132.1 7.7 %fusion.153 = (f32[2,512]{1,0:T(2,128)S(1)}, f32[2,512,2048]{2,1,0:T(8,128)}) fusion(pred[512,2048]{1,0:T(8,128)(4,1)S(1)} %broadcast_compare_fusion.4, bf16[2048,2,128]{2,0,1:T(8,128)(2,1)} %get-tuple-element.297, bf16[2,512,2,128]{3,1,0,2:T(8,128)(2,1)} %get-tuple-element.296, s32[]{:T(128)S(6)} %copy.93), kind=kOutput, calls=%fused_computation.161.clone.1 | convolution fusion | flops 545261568 | bytes 10752004 | tf_op jit(solution)/shard_map/while/body/eval_jaxpr/sub | solution.py:86
  139.7 5.0 %fusion.154 = bf16[1,512,2,128]{3,1,2,0:T(8,128)(2,1)S(1)} fusion(bf16[2048,2,128]{2,0,1:T(8,128)(2,1)} %get-tuple-element.298, f32[2,512,2048]{2,1,0:T(8,128)} %get-tuple-element.265, f32[2,512]{1,0:T(2,128)S(1)} %get-tuple-element.266), kind=kOutput, calls=%fused_computation.11.clone.1 | convolution fusion | flops 541196288 | bytes 9703424 | tf_op jit(solution)/shard_map/while/body/eval_jaxpr/hqk,khd->qhd/dot_general | solution.py:88
  145.7 7.7 %fusion.153 = (f32[2,512]{1,0:T(2,128)S(1)}, f32[2,512,2048]{2,1,0:T(8,128)}) fusion(pred[512,2048]{1,0:T(8,128)(4,1)S(1)} %broadcast_compare_fusion.4, bf16[2048,2,128]{2,0,1:T(8,128)(2,1)} %get-tuple-element.297, bf16[2,512,2,128]{3,1,0,2:T(8,128)(2,1)} %get-tuple-element.296, s32[]{:T(128)S(6)} %copy.93), kind=kOutput, calls=%fused_computation.161.clone.1 | convolution fusion | flops 545261568 | bytes 10752004 | tf_op jit(solution)/shard_map/while/body/eval_jaxpr/sub | solution.py:86
  153.4 4.9 %fusion.154 = bf16[1,512,2,128]{3,1,2,0:T(8,128)(2,1)S(1)} fusion(bf16[2048,2,128]{2,0,1:T(8,128)(2,1)} %get-tuple-element.298, f32[2,512,2048]{2,1,0:T(8,128)} %get-tuple-element.265, f32[2,512]{1,0:T(2,128)S(1)} %get-tuple-element.266), kind=kOutput, calls=%fused_computation.11.clone.1 | convolution fusion | flops 541196288 | bytes 9703424 | tf_op jit(solution)/shard_map/while/body/eval_jaxpr/hqk,khd->qhd/dot_general | solution.py:88
  158.6 1.1 reshape_reshape.9
  159.8 4.3 %all-to-all-start = ((bf16[8,128,256]{2,1,0:T(8,128)(2,1)}), bf16[8,128,256]{2,1,0:T(8,128)(2,1)}, u32[]{:S(2)}, u32[]{:S(2)}) async-start(bf16[8,128,256]{2,1,0:T(8,128)(2,1)} %reshape_reshape.9), calls=%async_computation | async-start | bytes 1048576 | tf_op jit(solution)/shard_map/all_to_all | solution.py:184
  164.0 1.4 fusion.124
  165.4 3.1 squeeze.33
  168.6 0.7 mul.226
  169.4 3.9 all-to-all-done
  173.3 7.0 %convert_reduce_fusion.1 = f32[128,3200]{1,0:T(8,128)S(1)} fusion(bf16[8,128,256]{2,1,0:T(8,128)(2,1)} %all-to-all-done, bf16[8,256,3200]{2,1,0:T(8,128)(2,1)} %bitcast.144), kind=kOutput, calls=%fused_computation.49 | convolution fusion | flops 1687142400 | bytes 15269888 | tf_op jit(solution)/shard_map/gtc,gcd->gtd/dot_general | solution.py:187
  180.3 2.2 reduce_sum.107
  182.5 3.1 fusion.112
  185.6 1.3 copy.47
  186.9 1.6 multiply_reduce_fusion.2
  189.1 2.8 reshape.367
  191.9 1.3 add_rsqrt_fusion.3
  193.2 1.3 rsqrt.56
  194.5 1.2 add_convert_fusion.3
  195.8 1.1 copy.48
  196.9 6.7 %all-to-all-start.1 = ((bf16[32,16,800]{2,0,1:T(8,128)(2,1)}), bf16[32,16,800]{2,0,1:T(8,128)(2,1)S(1)}, u32[]{:S(2)}, u32[]{:S(2)}) async-start(bf16[32,16,800]{2,0,1:T(8,128)(2,1)} %copy.48), calls=%async_computation.1 | async-start | bytes 1835008 | tf_op jit(solution)/shard_map/all_to_all | solution.py:228
  205.0 0.7 compare_convert_fusion
  205.7 0.7 broadcast_multiply_fusion.1
  206.4 1.1 copy.83
  207.5 10.1 %all-to-all-done.1 = bf16[32,16,800]{2,0,1:T(8,128)(2,1)S(1)} async-done(((bf16[32,16,800]{2,0,1:T(8,128)(2,1)}), bf16[32,16,800]{2,0,1:T(8,128)(2,1)S(1)}, u32[]{:S(2)}, u32[]{:S(2)}) %all-to-all-start.1) | async-done | bytes 819232 | tf_op jit(solution)/shard_map/all_to_all | solution.py:228
  218.0 12.5 %add_convert_fusion.1 = bf16[16,32,6144]{2,1,0:T(8,128)(2,1)} fusion(bf16[800,6144]{1,0:T(8,128)(2,1)} %param.27, f32[16,32]{1,0:T(8,128)S(1)} %get-tuple-element.180, bf16[16,32,800]{2,0,1:T(8,128)(2,1)S(1)} %convolution_convert_fusion.3), kind=kOutput, calls=%fused_computation.51 | convolution fusion | flops 5039456256 | bytes 16943104 | tf_op jit(solution)/shard_map/dot_general | solution.py:236
  231.3 0.8 copy.52
  232.4 27.3 %while.21 = (s32[]{:T(128)}, bf16[2,512,2,128]{3,2,1,0:T(2,128)(2,1)S(1)}, f32[2,512]{1,0:T(2,128)S(1)}, f32[1,2048]{1,0:T(1,128)S(1)}, bf16[2,512,2,128]{3,1,0,...) while((s32[]{:T(128)}, ...), condition=%wide.region_14.15_spmd, body=%wide.region_11.14_spmd.sunk | while | flops 1087506432 | bytes 22042728 | solution.py:92
  233.0 7.7 %fusion.158 = (f32[2,512]{1,0:T(2,128)S(1)}, f32[2,512,2048]{2,1,0:T(8,128)}) fusion(pred[512,2048]{1,0:T(8,128)(4,1)S(1)} %broadcast_compare_fusion.5, bf16[2048,2,128]{2,0,1:T(8,128)(2,1)} %get-tuple-element.321, bf16[2,512,2,128]{3,1,0,2:T(8,128)(2,1)} %get-tuple-element.320, s32[]{:T(128)S(6)} %copy.99), kind=kOutput, calls=%fused_computation.162.clone.1 | convolution fusion | flops 545261568 | bytes 10752004 | tf_op jit(solution)/shard_map/while/body/eval_jaxpr/sub | solution.py:86
  240.7 5.0 %fusion.159 = bf16[1,512,2,128]{3,1,2,0:T(8,128)(2,1)S(1)} fusion(bf16[2048,2,128]{2,0,1:T(8,128)(2,1)} %get-tuple-element.322, f32[2,512,2048]{2,1,0:T(8,128)} %get-tuple-element.274, f32[2,512]{1,0:T(2,128)S(1)} %get-tuple-element.275), kind=kOutput, calls=%fused_computation.35.clone.1 | convolution fusion | flops 541196288 | bytes 9703424 | tf_op jit(solution)/shard_map/while/body/eval_jaxpr/hqk,khd->qhd/dot_general | solution.py:88
  246.7 7.7 %fusion.158 = (f32[2,512]{1,0:T(2,128)S(1)}, f32[2,512,2048]{2,1,0:T(8,128)}) fusion(pred[512,2048]{1,0:T(8,128)(4,1)S(1)} %broadcast_compare_fusion.5, bf16[2048,2,128]{2,0,1:T(8,128)(2,1)} %get-tuple-element.321, bf16[2,512,2,128]{3,1,0,2:T(8,128)(2,1)} %get-tuple-element.320, s32[]{:T(128)S(6)} %copy.99), kind=kOutput, calls=%fused_computation.162.clone.1 | convolution fusion | flops 545261568 | bytes 10752004 | tf_op jit(solution)/shard_map/while/body/eval_jaxpr/sub | solution.py:86
  254.3 5.0 %fusion.159 = bf16[1,512,2,128]{3,1,2,0:T(8,128)(2,1)S(1)} fusion(bf16[2048,2,128]{2,0,1:T(8,128)(2,1)} %get-tuple-element.322, f32[2,512,2048]{2,1,0:T(8,128)} %get-tuple-element.274, f32[2,512]{1,0:T(2,128)S(1)} %get-tuple-element.275), kind=kOutput, calls=%fused_computation.35.clone.1 | convolution fusion | flops 541196288 | bytes 9703424 | tf_op jit(solution)/shard_map/while/body/eval_jaxpr/hqk,khd->qhd/dot_general | solution.py:88
  259.7 1.1 reshape_reshape.11
  260.8 7.0 %all-to-all-start.2 = ((bf16[8,128,256]{2,1,0:T(8,128)(2,1)}), bf16[8,128,256]{2,1,0:T(8,128)(2,1)}, u32[]{:S(2)}, u32[]{:S(2)}) async-start(bf16[8,128,256]{2,1,0:T(8,128)(2,1)} %reshape_reshape.11), calls=%async_computation.3 | async-start | bytes 1048576 | tf_op jit(solution)/shard_map/all_to_all | solution.py:184
  268.1 2.1 squeeze.38
  270.2 7.2 %all-to-all-done.2 = bf16[8,128,256]{2,1,0:T(8,128)(2,1)} async-done(((bf16[8,128,256]{2,1,0:T(8,128)(2,1)}), bf16[8,128,256]{2,1,0:T(8,128)(2,1)}, u32[]{:S(2)}, u32[]{:S(2)}) %all-to-all-start.2) | async-done | bytes 524320 | tf_op jit(solution)/shard_map/all_to_all | solution.py:184
  277.4 7.1 %convert_reduce_fusion = f32[128,3200]{1,0:T(8,128)S(1)} fusion(bf16[8,128,256]{2,1,0:T(8,128)(2,1)} %all-to-all-done.2, bf16[8,256,3200]{2,1,0:T(8,128)(2,1)} %bitcast.145), kind=kOutput, calls=%fused_computation.48 | convolution fusion | flops 1687142400 | bytes 15269888 | tf_op jit(solution)/shard_map/gtc,gcd->gtd/dot_general | solution.py:187
  284.6 2.2 reduce_sum.111
  286.8 2.6 fusion.111
  289.4 1.3 copy.55
  290.7 2.8 reshape.369
  293.6 1.0 multiply_reduce_fusion.1
  294.7 1.2 add_convert_fusion.2
  296.2 21.2 %all_to_all.36 = bf16[32,16,800]{2,0,1:T(8,128)(2,1)S(1)} all-to-all(bf16[32,16,800]{2,0,1:T(8,128)(2,1)S(1)} %copy.56), channel_id=1, replica_groups=mesh['rows'=16,'seq'=8] {'rows'}, dimensions={1} | all-to-all | bytes 1638400 | tf_op jit(solution)/shard_map/all_to_all | solution.py:228
  317.8 12.3 %add_convert_fusion = bf16[16,32,6144]{2,1,0:T(8,128)(2,1)} fusion(bf16[800,6144]{1,0:T(8,128)(2,1)} %param.27, f32[16,32]{1,0:T(8,128)S(1)} %copy-done.9, bf16[16,32,800]{2,0,1:T(8,128)(2,1)S(1)} %convolution_convert_fusion.2), kind=kOutput, calls=%fused_computation.50 | convolution fusion | flops 5039456256 | bytes 16943104 | tf_op jit(solution)/shard_map/dot_general | solution.py:236
  330.2 78.8 %reduce-scatter.5.cloned.1.call-done = bf16[32,6144]{1,0:T(8,128)(2,1)} async-done(((bf16[512,6144]{1,0:T(8,128)(2,1)}), bf16[32,6144]{1,0:T(8,128)(2,1)}) %reduce-scatter.5.cloned.1.call-update) | async-done | bytes 393232 | tf_op jit(solution)/shard_map/reduce_scatter | solution.py:202
  409.0 4.5 %fusion.76 = (bf16[32,6144]{1,0:T(8,128)(2,1)S(1)}, bf16[32,6144]{1,0:T(8,128)(2,1)S(1)}) fusion(bf16[32,6144]{1,0:T(8,128)(2,1)} %reduce-scatter.3.cloned.1.call-done, f32[6144]{0:T(1024)S(1)} %copy-done.7, bf16[32,6144]{1,0:T(8,128)(2,1)} %reduce-scatter.5.cloned.1.call-done), kind=kLoop, calls=%fused_computation.89 | loop fusion | flops 26345472 | bytes 1597440 | tf_op jit(solution)/shard_map/convert_element_type | solution.py:204
  413.5 0.9 maximum_bitcast_fusion
  (81 shorter events, 10.6 us)
Async XLA Ops:
  6.5 2.0 copy-start
  6.5 77.7 %all-gather.4.cloned.1.call-start = ((), (), s32[]{:S(2)}) async-start(), calls=%async_computation.6 | async-start | bytes 14745600 | tf_op jit(solution)/shard_map/all_gather | solution.py:124
  10.9 0.8 copy-start.13
  10.9 0.8 copy-start.10
  10.9 158.4 %all-gather.6.cloned.1.call-start = ((), (), s32[]{:S(2)}) async-start(), calls=%async_computation.9 | async-start | bytes 14745600 | tf_op jit(solution)/shard_map/all_gather | solution.py:158
  108.4 2.2 copy-start.2
  126.0 3.3 copy-start.1
  159.8 13.5 %all-to-all-start = ((bf16[8,128,256]{2,1,0:T(8,128)(2,1)}), bf16[8,128,256]{2,1,0:T(8,128)(2,1)}, u32[]{:S(2)}, u32[]{:S(2)}) async-start(bf16[8,128,256]{2,1,0:T(8,128)(2,1)} %reshape_reshape.9), calls=%async_computation | async-start | bytes 1048576 | tf_op jit(solution)/shard_map/all_to_all | solution.py:184
  165.4 3.1 copy-start.5
  165.4 3.2 copy-start.6
  180.3 2.2 copy-start.4
  195.8 7.9 %copy-start.14 = (s32[1,256]{1,0:T(1,128)S(1)}, s32[1,256]{1,0:T(1,128)}, u32[]{:S(2)}) copy-start(s32[1,256]{1,0:T(1,128)} %param.24) | copy-start | bytes 3076
  195.8 8.6 %copy-start.11 = (s32[16]{0:T(128)S(1)}, s32[16]{0:T(128)}, u32[]{:S(2)}) copy-start(s32[16]{0:T(128)} %param.29) | copy-start | bytes 196
  196.9 20.7 %all-to-all-start.1 = ((bf16[32,16,800]{2,0,1:T(8,128)(2,1)}), bf16[32,16,800]{2,0,1:T(8,128)(2,1)S(1)}, u32[]{:S(2)}, u32[]{:S(2)}) async-start(bf16[32,16,800]{2,0,1:T(8,128)(2,1)} %copy.48), calls=%async_computation.1 | async-start | bytes 1835008 | tf_op jit(solution)/shard_map/all_to_all | solution.py:228
  203.6 126.5 %reduce-scatter.3.cloned.1.call-start = ((), (), s32[]{:S(2)}) async-start(), calls=%async_computation.7 | async-start | bytes 6684672 | tf_op jit(solution)/shard_map/reduce_scatter | solution.py:202
  230.6 0.7 copy-start.8
  260.8 16.6 %all-to-all-start.2 = ((bf16[8,128,256]{2,1,0:T(8,128)(2,1)}), bf16[8,128,256]{2,1,0:T(8,128)(2,1)}, u32[]{:S(2)}, u32[]{:S(2)}) async-start(bf16[8,128,256]{2,1,0:T(8,128)(2,1)} %reshape_reshape.11), calls=%async_computation.3 | async-start | bytes 1048576 | tf_op jit(solution)/shard_map/all_to_all | solution.py:184
  267.8 141.2 %reduce-scatter.5.cloned.1.call-start = ((), (), s32[]{:S(2)}) async-start(), calls=%async_computation.8 | async-start | bytes 6684672 | tf_op jit(solution)/shard_map/reduce_scatter | solution.py:202
  284.6 2.2 copy-start.3
  296.0 21.4 %copy-start.12 = (s32[16]{0:T(128)S(1)}, s32[16]{0:T(128)}, u32[]{:S(2)}) copy-start(s32[16]{0:T(128)} %param.29) | copy-start | bytes 196
  296.2 21.6 %copy-start.9 = (f32[16,32]{1,0:T(8,128)S(1)}, f32[16,32]{1,0:T(8,128)}, u32[]{:S(2)}) copy-start(f32[16,32]{1,0:T(8,128)} %get-tuple-element.181) | copy-start | bytes 6148
  330.1 78.9 %copy-start.7 = (f32[6144]{0:T(1024)S(1)}, f32[6144]{0:T(1024)}, u32[]{:S(2)}) copy-start(f32[6144]{0:T(1024)} %param.28) | copy-start | bytes 73732
Sparse Core Ops, SparseCore 0:
  11.0 73.1 all-gather.3
  85.9 72.7 all-gather.5
  230.7 84.8 reduce-scatter.2
  330.3 78.6 reduce-scatter.4

commit v4 on v2

--- a/solution.py
+++ b/solution.py
@@ -68,6 +68,55 @@
         ],
         compiler_params=pltpu.CompilerParams(collective_id=0, has_side_effects=True),
     )(part)
+
+
+def rows_exchange_kernel(slab_ref, out_ref, send_sem, recv_sem):
+    n = out_ref.shape[0]
+    me = lax.axis_index("rows")
+    col = lax.axis_index("seq")
+    barrier = pltpu.get_barrier_semaphore()
+    for k in range(1, n):
+        peer = lax.rem(me + k, n)
+        pl.semaphore_signal(barrier, inc=1, device_id=(peer, col), device_id_type=MESH)
+    pl.semaphore_wait(barrier, n - 1)
+    sends = []
+    for k in range(1, n):
+        peer = lax.rem(me + k, n)
+        copy = pltpu.make_async_remote_copy(
+            src_ref=slab_ref.at[peer],
+            dst_ref=out_ref.at[me],
+            send_sem=send_sem.at[k],
+            recv_sem=recv_sem.at[me],
+            device_id=(peer, col),
+            device_id_type=MESH,
+        )
+        copy.start()
+        sends.append(copy)
+    out_ref[me] = slab_ref[me]
+    for k in range(1, n):
+        src = lax.rem(me + n - k, n)
+        pltpu.make_async_remote_copy(
+            src_ref=slab_ref.at[src],
+            dst_ref=out_ref.at[src],
+            send_sem=send_sem.at[k],
+            recv_sem=recv_sem.at[src],
+            device_id=(src, col),
+            device_id_type=MESH,
+        ).wait_recv()
+    for copy in sends:
+        copy.wait_send()
+
+
+def rows_exchange(slabs):
+    n = slabs.shape[0]
+    return pl.pallas_call(
+        rows_exchange_kernel,
+        out_shape=jax.ShapeDtypeStruct(slabs.shape, slabs.dtype),
+        in_specs=[pl.BlockSpec(memory_space=pltpu.VMEM)],
+        out_specs=pl.BlockSpec(memory_space=pltpu.VMEM),
+        scratch_shapes=[pltpu.SemaphoreType.DMA((n,)), pltpu.SemaphoreType.DMA((n,))],
+        compiler_params=pltpu.CompilerParams(collective_id=1, has_side_effects=True),
+    )(slabs)
 
 
 def attend_dense(query_norm, key_norm, value_half, row_segments, block_len, scale):
@@ -176,15 +225,17 @@
     centre = merged - jnp.mean(merged, axis=-1, keepdims=True)
     spread = jnp.mean(centre * centre, axis=-1, keepdims=True)
     merged_norm = (centre * lax.rsqrt(spread + 1e-05) * ln_weight + ln_bias).astype(jnp.bfloat16)
+    row_count = lax.axis_size("rows")
+    row_me = lax.axis_index("rows")
     merged_mask = (
         pad_mask[0]
         .reshape(lines, 2, half_grid, 2)[:, 0, :, 0]
         .reshape(merged_count)
         .astype(jnp.float32)
     )
-    row_count = lax.axis_size("rows")
-    row_me = lax.axis_index("rows")
-    slabs = lax.all_to_all(merged_norm, "rows", split_axis=1, concat_axis=0, tiled=True)
+    slabs = rows_exchange(
+        jnp.transpose(merged_norm.reshape(merged_count, row_count, -1), (1, 0, 2))
+    )
     owner_hot = (owner[None, :] == jnp.arange(row_count, dtype=jnp.int32)[:, None]).astype(
         jnp.bfloat16
     )

time: 392 us -> 400 us (1.020)
  Pallas kernels: 11.6 us -> 44.1 us
  waiting for transfers between devices: 200 us -> 181 us
  starting transfers between devices: 10.7 us -> 3.88 us
    pallas_call x0 -> x1, Pallas kernels: none -> 32.5 us  [rows_exchange(): pl.pallas_call(rows_exchange_kernel, out_shape=jax.ShapeDtypeStruct(slabs...]
    all_to_all x1 -> x0, waiting for transfers between devices: 20.2 us -> none  [per_device(): lax.all_to_all(merged_norm, 'rows', split_axis=1, concat_axis=0, tiled=True)]
    all_to_all x1 -> x0, starting transfers between devices: 6.83 us -> none  [per_device(): lax.all_to_all(merged_norm, 'rows', split_axis=1, concat_axis=0, tiled=True)]
    transpose x0 -> x1, other arithmetic: none -> 4.65 us  [per_device(): jnp.transpose(merged_norm.reshape(merged_count, row_count, -1), (1, 0, 2))]
  transfers between devices with their start and end apart: 5 -> 4, of which waited for: 4 -> 3; matrix products, arithmetic and copies ran while one was open for 24% -> 23% of each run, Pallas kernels for 3% -> 3%
where the time goes in v4:
time: 400 us; the launch traced here: 399 us
  waiting for transfers between devices  181 us (45%)
  matrix products  98.1 us (25%)
  Pallas kernels  44.1 us (11%)
  other arithmetic  31 us (8%)
  local copies, waits for them, and re-layouts  27.6 us (7%)
  between operations  13.3 us (3%)
    reduce_scatter x1, waiting for transfers between devices, per_device(): lax.psum_scatter(partial.reshape(row_count * merged_count, -1), 'rows', s...  99 us
    all_gather x1, waiting for transfers between devices, per_device(): row_tokens = lax.all_gather(normed, 'seq', axis=0, tiled=True)  72.5 us
    pallas_call x1, Pallas kernels, rows_exchange(): pl.pallas_call(rows_exchange_kernel, out_shape=jax.ShapeDtypeStruct(slabs...  32.5 us
    sub x4, matrix products, one_block(): exp_terms = jnp.exp(scores - peak_val)  31 us
    dot_general x1, matrix products, per_device(): jnp.dot(ordered, fc_weight, preferred_element_type=jnp.float32)  19.2 us
    dot_general x4, matrix products, one_block(): jnp.einsum('hqk,khd->qhd', probs, value_half, preferred_element_type=jnp....  18.9 us
    dot_general x1, matrix products, per_device(): jnp.dot(row_tokens, qkv_weight, preferred_element_type=jnp.float32)  15.7 us
    pallas_call x1, Pallas kernels, seq_sum(): pl.pallas_call(seq_sum_kernel, out_shape=jax.ShapeDtypeStruct(part.shape,...  11.6 us
  transfers between devices with their start and end apart: 4, of which 3 were waited for; matrix products, arithmetic and copies ran while one was open for 23% of the time, Pallas kernels for 3%

profile of v4, /device:TPU:1, one launch (start us, length us, event | category | flops | bytes accessed | tf_op | source)
XLA Modules:
  0.0 399.3 jit_solution(15400333762405657574)
XLA Ops:
  6.5 2.0 fusion.32
  8.5 2.4 fusion.34
  10.9 0.0 all-gather.6.cloned.1.call-start
  11.0 0.7 all-gather.6.cloned.1.call-update
  11.7 72.5 %all-gather.4.cloned.1.call-done = bf16[2048,3200]{1,0:T(8,128)(2,1)} async-done(((bf16[256,3200]{1,0:T(8,128)(2,1)}), bf16[2048,3200]{1,0:T(8,128)(2,1)}) %all-gather.4.cloned.1.call-update) | async-done | bytes 13107216 | tf_op jit(solution)/shard_map/all_gather | solution.py:173
  84.2 15.7 %fusion.73 = f32[2048,768]{0,1:T(8,128)S(1)} fusion(bf16[2048,3200]{1,0:T(8,128)(2,1)} %all-gather.4.cloned.1.call-done, bf16[3200,768]{1,0:T(8,128)(2,1)} %param.17), kind=kOutput, calls=%fused_computation.96 | convolution fusion | flops 10066329600 | bytes 24313856 | tf_op jit(solution)/shard_map/dot_general | solution.py:176
  99.9 0.1 slice.41
  100.1 2.5 fusion.71
  102.5 1.9 copy.38
  104.4 2.9 copy.37
  107.3 0.3 fusion.35
  107.7 1.3 copy-done
  108.9 0.3 multiply_reduce_fusion.1
  109.3 0.6 pad_maximum_fusion.part_ref
  109.9 11.6 %shard_map.127 = f32[3,2048]{1,0:T(4,128)} custom-call(f32[3,2048]{1,0:T(4,128)} %pad_maximum_fusion.part_ref), custom_call_target="tpu_custom_call" | custom-call | tf_op jit(solution)/shard_map/pallas_call | solution.py:59
  121.6 0.9 rsqrt_reduce_fusion
  122.5 1.3 copy.39
  123.9 3.0 multiply_convert_fusion
  126.8 1.3 fusion.37
  128.1 53.8 %while.10 = (s32[]{:T(128)}, bf16[4,512,2,128]{3,2,1,0:T(2,128)(2,1)S(1)}, f32[4,512]{1,0:T(4,128)S(1)}, f32[1,2048]{1,0:T(1,128)S(1)}, bf16[4,512,2,128]{3,1,0,...) while((s32[]{:T(128)}, ...), condition=%wide.region_6.7_spmd, body=%wide.region_3.6_spmd.sunk | while | flops 1087506432 | bytes 26237560 | solution.py:141
  128.1 0.7 broadcast_compare_fusion.2
  128.8 7.7 %fusion.89 = (f32[2,512]{1,0:T(2,128)S(1)}, f32[2,512,2048]{2,1,0:T(8,128)}) fusion(pred[512,2048]{1,0:T(8,128)(4,1)S(1)} %broadcast_compare_fusion.2, bf16[2048,2,128]{2,0,1:T(8,128)(2,1)} %get-tuple-element.151, bf16[4,512,2,128]{3,1,0,2:T(8,128)(2,1)} %get-tuple-element.150, s32[]{:T(128)} %get-tuple-element.138), kind=kOutput, calls=%fused_computation.93.clone.1 | convolution fusion | flops 545261568 | bytes 10752512 | tf_op jit(solution)/shard_map/while/body/eval_jaxpr/sub | solution.py:135
  136.5 4.7 %fusion.90 = bf16[1,512,2,128]{3,1,2,0:T(8,128)(2,1)S(1)} fusion(bf16[2048,2,128]{2,0,1:T(8,128)(2,1)S(1)} %copy-done.5, f32[2,512,2048]{2,1,0:T(8,128)} %get-tuple-element.128, f32[2,512]{1,0:T(2,128)S(1)} %get-tuple-element.129), kind=kOutput, calls=%fused_computation.11.clone.1 | convolution fusion | flops 541196288 | bytes 9703424 | tf_op jit(solution)/shard_map/while/body/eval_jaxpr/hqk,khd->qhd/dot_general | solution.py:137
  141.2 0.3 copy_dynamic-update-slice_fusion.2
  141.6 0.7 broadcast_compare_fusion.2
  142.2 7.7 %fusion.89 = (f32[2,512]{1,0:T(2,128)S(1)}, f32[2,512,2048]{2,1,0:T(8,128)}) fusion(pred[512,2048]{1,0:T(8,128)(4,1)S(1)} %broadcast_compare_fusion.2, bf16[2048,2,128]{2,0,1:T(8,128)(2,1)} %get-tuple-element.151, bf16[4,512,2,128]{3,1,0,2:T(8,128)(2,1)} %get-tuple-element.150, s32[]{:T(128)} %get-tuple-element.138), kind=kOutput, calls=%fused_computation.93.clone.1 | convolution fusion | flops 545261568 | bytes 10752512 | tf_op jit(solution)/shard_map/while/body/eval_jaxpr/sub | solution.py:135
  150.0 4.8 %fusion.90 = bf16[1,512,2,128]{3,1,2,0:T(8,128)(2,1)S(1)} fusion(bf16[2048,2,128]{2,0,1:T(8,128)(2,1)S(1)} %copy-done.5, f32[2,512,2048]{2,1,0:T(8,128)} %get-tuple-element.128, f32[2,512]{1,0:T(2,128)S(1)} %get-tuple-element.129), kind=kOutput, calls=%fused_computation.11.clone.1 | convolution fusion | flops 541196288 | bytes 9703424 | tf_op jit(solution)/shard_map/while/body/eval_jaxpr/hqk,khd->qhd/dot_general | solution.py:137
  154.8 0.3 copy_dynamic-update-slice_fusion.2
  155.1 0.7 broadcast_compare_fusion.2
  155.8 7.7 %fusion.89 = (f32[2,512]{1,0:T(2,128)S(1)}, f32[2,512,2048]{2,1,0:T(8,128)}) fusion(pred[512,2048]{1,0:T(8,128)(4,1)S(1)} %broadcast_compare_fusion.2, bf16[2048,2,128]{2,0,1:T(8,128)(2,1)} %get-tuple-element.151, bf16[4,512,2,128]{3,1,0,2:T(8,128)(2,1)} %get-tuple-element.150, s32[]{:T(128)} %get-tuple-element.138), kind=kOutput, calls=%fused_computation.93.clone.1 | convolution fusion | flops 545261568 | bytes 10752512 | tf_op jit(solution)/shard_map/while/body/eval_jaxpr/sub | solution.py:135
  163.5 4.7 %fusion.90 = bf16[1,512,2,128]{3,1,2,0:T(8,128)(2,1)S(1)} fusion(bf16[2048,2,128]{2,0,1:T(8,128)(2,1)S(1)} %copy-done.5, f32[2,512,2048]{2,1,0:T(8,128)} %get-tuple-element.128, f32[2,512]{1,0:T(2,128)S(1)} %get-tuple-element.129), kind=kOutput, calls=%fused_computation.11.clone.1 | convolution fusion | flops 541196288 | bytes 9703424 | tf_op jit(solution)/shard_map/while/body/eval_jaxpr/hqk,khd->qhd/dot_general | solution.py:137
  168.2 0.3 copy_dynamic-update-slice_fusion.2
  168.5 0.7 broadcast_compare_fusion.2
  169.2 7.7 %fusion.89 = (f32[2,512]{1,0:T(2,128)S(1)}, f32[2,512,2048]{2,1,0:T(8,128)}) fusion(pred[512,2048]{1,0:T(8,128)(4,1)S(1)} %broadcast_compare_fusion.2, bf16[2048,2,128]{2,0,1:T(8,128)(2,1)} %get-tuple-element.151, bf16[4,512,2,128]{3,1,0,2:T(8,128)(2,1)} %get-tuple-element.150, s32[]{:T(128)} %get-tuple-element.138), kind=kOutput, calls=%fused_computation.93.clone.1 | convolution fusion | flops 545261568 | bytes 10752512 | tf_op jit(solution)/shard_map/while/body/eval_jaxpr/sub | solution.py:135
  177.0 4.7 %fusion.90 = bf16[1,512,2,128]{3,1,2,0:T(8,128)(2,1)S(1)} fusion(bf16[2048,2,128]{2,0,1:T(8,128)(2,1)S(1)} %copy-done.5, f32[2,512,2048]{2,1,0:T(8,128)} %get-tuple-element.128, f32[2,512]{1,0:T(2,128)S(1)} %get-tuple-element.129), kind=kOutput, calls=%fused_computation.11.clone.1 | convolution fusion | flops 541196288 | bytes 9703424 | tf_op jit(solution)/shard_map/while/body/eval_jaxpr/hqk,khd->qhd/dot_general | solution.py:137
  181.6 0.3 copy_dynamic-update-slice_fusion.2
  182.0 1.5 reshape_reshape.3
  183.5 3.8 all-to-all-start
  187.3 3.0 reshape.210
  190.4 0.1 add.95
  190.5 0.1 mul.171
  190.6 0.5 broadcast.188
  191.1 0.7 reduce.16
  191.7 0.1 reshape_squeeze.8
  191.9 0.1 fusion.61
  192.0 0.1 mul.177
  192.1 0.6 dynamic_slice.11
  192.7 0.6 compare_convert_fusion
  193.3 0.1 broadcast_multiply_fusion
  193.4 9.0 %all-to-all-done = bf16[8,256,256]{2,1,0:T(8,128)(2,1)S(1)} async-done(((bf16[8,256,256]{2,1,0:T(8,128)(2,1)}), bf16[8,256,256]{2,1,0:T(8,128)(2,1)S(1)}, u32[]{:S(2)}, u32[]{:S(2)}) %all-to-all-start) | async-done | bytes 1048608 | tf_op jit(solution)/shard_map/all_to_all | solution.py:210
  202.3 10.6 %convert_reduce_fusion = f32[256,3200]{1,0:T(8,128)} fusion(bf16[8,256,256]{2,1,0:T(8,128)(2,1)S(1)} %all-to-all-done, bf16[8,256,3200]{2,1,0:T(8,128)(2,1)} %bitcast.96), kind=kOutput, calls=%fused_computation.24 | convolution fusion | flops 3374284800 | bytes 17432576 | tf_op jit(solution)/shard_map/gtc,gcd->gtd/dot_general | solution.py:214
  212.9 5.3 %reduce_sum.69 = f32[4,2,16,2,3200]{4,3,2,1,0:T(2,128)} reshape(f32[256,3200]{1,0:T(8,128)} %convert_reduce_fusion) | data formatting | bytes 6553600 | tf_op jit(solution)/shard_map/reduce_sum | solution.py:217
  218.3 4.2 %fusion.65 = (f32[4,16]{1,0:T(4,128)S(1)}, f32[4,16,2,2,3200]{4,3,1,2,0:T(2,128)S(1)}) fusion(f32[4,2,16,2,3200]{4,3,2,1,0:T(2,128)S(1)} %copy-done.3, f32[4,2,16,2,3200]{4,3,2,1,0:T(2,128)} %reduce_sum.69, f32[3200]{0:T(1024)S(1)} %copy-done.9), kind=kLoop, calls=%fused_computation.92 | loop fusion | flops 2457536 | bytes 9843456 | tf_op jit(solution)/shard_map/reduce_sum | solution.py:225
  222.5 0.3 copy.30
  222.8 1.9 multiply_reduce_fusion
  224.7 0.1 div.33
  224.8 0.1 rsqrt.45
  224.9 4.5 %reshape.208 = f32[64,16,800]{2,1,0:T(8,128)} reshape(f32[4,16,2,2,3200]{4,3,2,1,0:T(2,128)S(1)} %copy.30) | data formatting | bytes 6553600 | tf_op jit(solution)/shard_map/reshape | solution.py:222
  229.3 4.7 %fusion.38.slab_ref = bf16[16,64,800]{2,1,0:T(8,128)(2,1)} fusion(f32[64,16,800]{2,1,0:T(8,128)} %reshape.208, f32[16,800]{1,0:T(8,128)S(1)} %add.95, f32[16,800]{1,0:T(8,128)S(1)} %mul.171, f32[64]{0:T(128)S(1)} %rsqrt.45, f32[64]{0:T(128)S(1)} %div.33), kind=kLoop, calls=%fused_computation.47 | loop fusion | flops 4096000 | bytes 5018112 | tf_op jit(solution)/shard_map/transpose | solution.py:237
  234.0 32.5 %shard_map.128 = bf16[16,64,800]{2,1,0:T(8,128)(2,1)} custom-call(bf16[16,64,800]{2,1,0:T(8,128)(2,1)} %fusion.38.slab_ref), custom_call_target="tpu_custom_call" | custom-call | tf_op jit(solution)/shard_map/pallas_call | solution.py:112
  266.5 2.7 fusion.42
  269.2 19.2 %add_convert_fusion = bf16[16,64,6144]{2,1,0:T(8,128)(2,1)} fusion(f32[16,64]{1,0:T(8,128)S(1)} %broadcast_multiply_fusion, bf16[800,6144]{1,0:T(8,128)(2,1)} %param.25, bf16[16,64,800]{2,0,1:T(8,128)(2,1)S(1)} %fusion.42), kind=kOutput, calls=%fused_computation.25 | convolution fusion | flops 10078912512 | bytes 24055808 | tf_op jit(solution)/shard_map/dot_general | solution.py:249
  288.5 99.0 %reduce-scatter.2.cloned.1.call-done = bf16[64,6144]{1,0:T(8,128)(2,1)} async-done(((bf16[1024,6144]{1,0:T(8,128)(2,1)}), bf16[64,6144]{1,0:T(8,128)(2,1)}) %reduce-scatter.2.cloned.1.call-update) | async-done | bytes 786448 | tf_op jit(solution)/shard_map/reduce_scatter | solution.py:255
  387.6 5.2 %fusion.58 = bf16[1,64,6144]{2,1,0:T(8,128)(2,1)} fusion(bf16[64,6144]{1,0:T(8,128)(2,1)} %reduce-scatter.2.cloned.1.call-done, f32[6144]{0:T(1024)S(1)} %copy-done.8), kind=kLoop, calls=%fused_computation.74 | loop fusion | flops 26345472 | bytes 1597440 | tf_op jit(solution)/shard_map/broadcast_in_dim | solution.py:262
  (51 shorter events, 0.2 us)
Async XLA Ops:
  6.5 2.0 copy-start.1
  6.5 77.7 %all-gather.4.cloned.1.call-start = ((), (), s32[]{:S(2)}) async-start(), calls=%async_computation.2 | async-start | bytes 14745600 | tf_op jit(solution)/shard_map/all_gather | solution.py:173
  10.9 0.8 copy-start.11
  10.9 0.8 copy-start.10
  10.9 182.5 %all-gather.6.cloned.1.call-start = ((), (), s32[]{:S(2)}) async-start(), calls=%async_computation.4 | async-start | bytes 14745600 | tf_op jit(solution)/shard_map/all_gather | solution.py:213
  107.3 1.6 copy-start
  126.8 1.3 copy-start.4
  128.8 7.7 %copy-start.5 = (bf16[2048,2,128]{2,0,1:T(8,128)(2,1)S(1)}, bf16[2048,2,128]{2,0,1:T(8,128)(2,1)}, u32[]{:S(2)}) copy-start(bf16[2048,2,128]{2,0,1:T(8,128)(2,1)} %get-tuple-element.152) | copy-start | bytes 3145732 | tf_op jit(solution)/shard_map/while
  142.2 7.8 %copy-start.5 = (bf16[2048,2,128]{2,0,1:T(8,128)(2,1)S(1)}, bf16[2048,2,128]{2,0,1:T(8,128)(2,1)}, u32[]{:S(2)}) copy-start(bf16[2048,2,128]{2,0,1:T(8,128)(2,1)} %get-tuple-element.152) | copy-start | bytes 3145732 | tf_op jit(solution)/shard_map/while
  155.8 7.8 %copy-start.5 = (bf16[2048,2,128]{2,0,1:T(8,128)(2,1)S(1)}, bf16[2048,2,128]{2,0,1:T(8,128)(2,1)}, u32[]{:S(2)}) copy-start(bf16[2048,2,128]{2,0,1:T(8,128)(2,1)} %get-tuple-element.152) | copy-start | bytes 3145732 | tf_op jit(solution)/shard_map/while
  169.2 7.8 %copy-start.5 = (bf16[2048,2,128]{2,0,1:T(8,128)(2,1)S(1)}, bf16[2048,2,128]{2,0,1:T(8,128)(2,1)}, u32[]{:S(2)}) copy-start(bf16[2048,2,128]{2,0,1:T(8,128)(2,1)} %get-tuple-element.152) | copy-start | bytes 3145732 | tf_op jit(solution)/shard_map/while
  181.9 5.4 %copy-start.2 = (bf16[1,256,3200]{2,1,0:T(8,128)(2,1)S(1)}, bf16[1,256,3200]{2,1,0:T(8,128)(2,1)}, u32[]{:S(2)}) copy-start(bf16[1,256,3200]{2,1,0:T(8,128)(2,1)} %param.15) | copy-start | bytes 4915204
  183.5 18.9 %all-to-all-start = ((bf16[8,256,256]{2,1,0:T(8,128)(2,1)}), bf16[8,256,256]{2,1,0:T(8,128)(2,1)S(1)}, u32[]{:S(2)}, u32[]{:S(2)}) async-start(bf16[8,256,256]{2,1,0:T(8,128)(2,1)} %reshape_reshape.3), calls=%async_computation | async-start | bytes 2097152 | tf_op jit(solution)/shard_map/all_to_all | solution.py:210
  187.2 3.1 copy-start.6
  187.3 3.2 copy-start.7
  187.3 3.8 copy-start.12
  187.3 4.8 %copy-start.13 = (s32[16]{0:T(128)S(1)}, s32[16]{0:T(128)}, u32[]{:S(2)}) copy-start(s32[16]{0:T(128)} %param.27) | copy-start | bytes 196
  187.3 200.3 %reduce-scatter.2.cloned.1.call-start = ((), (), s32[]{:S(2)}) async-start(), calls=%async_computation.3 | async-start | bytes 13369344 | tf_op jit(solution)/shard_map/reduce_scatter | solution.py:255
  212.9 5.3 %copy-start.3 = (f32[4,2,16,2,3200]{4,3,2,1,0:T(2,128)S(1)}, f32[4,2,16,2,3200]{4,3,2,1,0:T(2,128)}, u32[]{:S(2)}) copy-start(f32[4,2,16,2,3200]{4,3,2,1,0:T(2,128)} %reshape.210) | copy-start | bytes 9830404
  212.9 5.3 %copy-start.9 = (f32[3200]{0:T(1024)S(1)}, f32[3200]{0:T(1024)}, u32[]{:S(2)}) copy-start(f32[3200]{0:T(1024)} %param.20) | copy-start | bytes 38404
  288.5 99.1 %copy-start.8 = (f32[6144]{0:T(1024)S(1)}, f32[6144]{0:T(1024)}, u32[]{:S(2)}) copy-start(f32[6144]{0:T(1024)} %param.26) | copy-start | bytes 73732
Sparse Core Ops, SparseCore 0:
  11.0 73.1 all-gather.3
  85.9 72.7 all-gather.5
  288.6 98.8 reduce-scatter.1
